TPU v7x, 32 devices: a whole 2x2x4 slice. The times are simulated.
32 devices in a mesh: grp: 2 (over y), seq: 4 (over z), head: 2 (over x), rep: 2 (over core).
Axes of the slice: x: 2, y: 2, z: 4, core: 2. Of those that a mesh axis runs over, the one named last changes fastest.
Arguments:
- query_latent: bfloat16 [1024, 32, 512], P(('grp', 'seq'), ('head', 'rep')), parts along dimension 0, may hold values from -400 to 400
- query_rope: bfloat16 [1024, 2048], P(('grp', 'seq'), ('head', 'rep')), parts along dimension 0, may hold values from -4 to 4
- latent: bfloat16 [8192, 512], P(('grp', 'seq', 'rep')), parts along dimension 0, may hold values from -6 to 6
- key_rope: bfloat16 [64, 8192], P(None, ('grp', 'seq', 'rep')), parts along dimension 1, may hold values from -4 to 4
- value_up: bfloat16 [32, 512, 128], P(('head', 'rep')), may hold values from -2.390625 to 2.390625
- out_proj: bfloat16 [4096, 3584], P(('head', 'rep')), may hold values from -0.09375 to 0.09375
Outputs:
- output: bfloat16 [1024, 3584], P(('grp', 'seq', 'head', 'rep')), parts along dimension 0
There are 2 independent parts, one for each index of `grp`. A program takes and returns all parts, laid end to end along the dimension named above; an argument that names none is the same for every part. Nothing has to cross between parts.
All inputs are finite; a program needn't handle non-finite values.
Results may differ from a plain program's by a relative error of at most 0.017.
Values may be sent and summed in bfloat16 or wider, within the bound.
No kernel may reach another device: no remote copies, remote signals or barrier semaphores. Data moves between devices by JAX's collectives and lax.ppermute only.
A program may use at most 128 MiB of HBM per device.

v0:
```python
import jax
import jax.numpy as jnp
from jax import lax
from jax.sharding import PartitionSpec as P

masked_score = -1e30


def shifted(value, axis, by):
    peers = lax.axis_size(axis)
    pairs = [(i, i + by) for i in range(peers) if 0 <= i + by < peers]
    return lax.ppermute(value, axis, pairs)


def fetch_partners(key_pair, levels):
    fetched = []
    current = key_pair
    for level_index in range(levels):
        current = shifted((key_pair[0], key_pair[1]), "seq", 2**level_index)
        fetched.append(current)
    return fetched


def attend_block(carry_state, query_latent, rope_queries, block, allowed, score_scale):
    running_max, running_sum, running_out = carry_state
    block_latent, block_rope = block
    scores = jnp.einsum(
        "qhc,kc->hqk", query_latent, block_latent, preferred_element_type=jnp.float32
    )
    scores = scores + jnp.einsum(
        "qhr,rk->hqk", rope_queries, block_rope, preferred_element_type=jnp.float32
    )
    scores = jnp.where(allowed, scores * score_scale, masked_score)
    new_max = jnp.maximum(running_max, jnp.max(scores, axis=2, keepdims=True))
    weights = jnp.exp(scores - new_max)
    factor = jnp.exp(running_max - new_max)
    running_sum = running_sum * factor + jnp.sum(weights, axis=2, keepdims=True)
    update = jnp.einsum(
        "hqk,kc->hqc",
        weights.astype(jnp.bfloat16),
        block_latent,
        preferred_element_type=jnp.float32,
    )
    return (new_max, running_sum, running_out * factor + update)


def shards(query_latent, query_rope, latent, key_rope, value_up, out_proj):
    query_rows, heads_here, latent_width = query_latent.shape
    rope_width = key_rope.shape[0]
    levels = min(4, lax.axis_size("seq") // 4 + 1)
    shard_index = lax.axis_index("seq")
    score_scale = (latent_width + rope_width) ** (-0.5)
    rope_queries = query_rope.reshape(query_rows, heads_here, rope_width)
    partners = fetch_partners((latent, key_rope), levels)
    stacked_latent = jnp.stack([latent] + [partner[0] for partner in partners])
    stacked_rope = jnp.stack([key_rope] + [partner[1] for partner in partners])
    block_latent, block_rope = (
        lax.all_gather(stacked_latent, "rep", axis=1, tiled=True),
        lax.all_gather(stacked_rope, "rep", axis=2, tiled=True),
    )
    blocks = [
        (block_latent[level_index], block_rope[level_index]) for level_index in range(levels + 1)
    ]
    block_rows = blocks[0][0].shape[0]
    key_index = jnp.arange(block_rows, dtype=jnp.int32)
    query_index = jnp.arange(query_rows, dtype=jnp.int32)
    causal = key_index[None, None, :] <= (block_rows - query_rows + query_index)[None, :, None]
    carry_state = (
        jnp.full((heads_here, query_rows, 1), masked_score, jnp.float32),
        jnp.zeros((heads_here, query_rows, 1), jnp.float32),
        jnp.zeros((heads_here, query_rows, latent_width), jnp.float32),
    )
    carry_state = attend_block(
        carry_state, query_latent, rope_queries, blocks[0], causal, score_scale
    )
    for level_index in range(levels):
        present = shard_index >= 2**level_index
        carry_state = attend_block(
            carry_state, query_latent, rope_queries, blocks[level_index + 1], present, score_scale
        )
    attended = (carry_state[2] / carry_state[1]).astype(jnp.bfloat16)
    expanded = jnp.einsum(
        "hqc,hcv->qhv", attended, value_up, preferred_element_type=jnp.float32
    ).astype(jnp.bfloat16)
    expanded = expanded.reshape(query_rows, heads_here * value_up.shape[2])
    return lax.psum_scatter(
        jnp.dot(expanded, out_proj, preferred_element_type=jnp.float32).astype(jnp.bfloat16),
        ("head", "rep"),
        scatter_dimension=0,
        tiled=True,
    )


def solution(mesh):
    placed = (
        P(("grp", "seq"), ("head", "rep"), None),
        P(("grp", "seq"), ("head", "rep")),
        P(("grp", "seq", "rep"), None),
        P(None, ("grp", "seq", "rep")),
        P(("head", "rep"), None, None),
        P(("head", "rep"), None),
    )
    return jax.shard_map(
        shards,
        mesh=mesh,
        in_specs=placed,
        out_specs=P(("grp", "seq", "head", "rep"), None),
        check_vma=False,
    )
```

profile of v0, /device:TPU:0, one launch (start us, length us, event | category | flops | bytes accessed | tf_op | source)
XLA Modules:
  0.0 120.0 jit_solution(14308483013304031724)
XLA Ops:
  6.5 0.0 copy-start
  6.5 0.0 copy-start.4
  6.5 0.0 copy-start.3
  6.5 0.0 all-gather.2.cloned.1.call-start
  6.5 6.1 %collective-permute-start.1 = (bf16[512,512]{1,0:T(8,128)(2,1)}, bf16[512,512]{1,0:T(8,128)(2,1)S(1)}, u32[]{:S(2)}, u32[]{:S(2)}) collective-permute-start(bf16[512,512]{1,0:T(8,128)(2,1)} %param.8), channel_id=1, source_target_pairs={{0,8},{4,12},{1,9},{5,13},{2,10},{6,14},{3,11},{7,15},{16,24},{20,... | collective-permute-start | bytes 1572872 | tf_op jit(solution)/shard_map/ppermute | solution.py:12
  12.7 3.5 %collective-permute-start = (bf16[512,512]{1,0:T(8,128)(2,1)}, bf16[512,512]{1,0:T(8,128)(2,1)S(1)}, u32[]{:S(2)}, u32[]{:S(2)}) collective-permute-start(bf16[512,512]{1,0:T(8,128)(2,1)} %param.8), channel_id=1, source_target_pairs={{0,4},{4,8},{8,12},{1,5},{5,9},{9,13},{2,6},{6,10},{10,14},{3,7},{... | collective-permute-start | bytes 1572872 | tf_op jit(solution)/shard_map/ppermute | solution.py:12
  16.2 9.1 %collective-permute-done.1 = bf16[512,512]{1,0:T(8,128)(2,1)S(1)} collective-permute-done((bf16[512,512]{1,0:T(8,128)(2,1)}, bf16[512,512]{1,0:T(8,128)(2,1)S(1)}, u32[]{:S(2)}, u32[]{:S(2)}) %collective-permute-start.1) | collective-permute-done | bytes 524320 | tf_op jit(solution)/shard_map/ppermute | solution.py:12
  25.3 10.1 %collective-permute-done = bf16[512,512]{1,0:T(8,128)(2,1)S(1)} collective-permute-done((bf16[512,512]{1,0:T(8,128)(2,1)}, bf16[512,512]{1,0:T(8,128)(2,1)S(1)}, u32[]{:S(2)}, u32[]{:S(2)}) %collective-permute-start) | collective-permute-done | bytes 524320 | tf_op jit(solution)/shard_map/ppermute | solution.py:12
  35.4 2.4 %pad_maximum_fusion = bf16[3,512,512]{2,1,0:T(8,128)(2,1)} fusion(bf16[1,512,512]{2,1,0:T(8,128)(2,1)S(1)} %bitcast.77, bf16[1,512,512]{2,1,0:T(8,128)(2,1)S(1)} %bitcast.78, bf16[1,512,512]{2,1,0:T(8,128)(2,1)} %bitcast.76), kind=kLoop, calls=%fused_computation.24 | loop fusion | flops 1572864 | bytes 3145728 | tf_op jit(solution)/shard_map/stack | solution.py:55
  37.8 0.0 all-gather.2.cloned.1.call-update
  37.8 0.0 reduce-scatter.2.cloned.1.call-start
  37.9 0.0 copy-done.4
  37.9 16.4 %collective-permute-start.3 = (bf16[64,512]{1,0:T(8,128)(2,1)S(1)}, bf16[64,512]{1,0:T(8,128)(2,1)S(1)}, u32[]{:S(2)}, u32[]{:S(2)}) collective-permute-start(bf16[64,512]{1,0:T(8,128)(2,1)S(1)} %copy-done.4), channel_id=1, source_target_pairs={{0,8},{4,12},{1,9},{5,13},{2,10},{6,14},{3,11},{7,15},{16,24},{20,... | collective-permute-start | bytes 196616 | tf_op jit(solution)/shard_map/ppermute | solution.py:12
  54.3 1.3 %collective-permute-start.2 = (bf16[64,512]{1,0:T(8,128)(2,1)S(1)}, bf16[64,512]{1,0:T(8,128)(2,1)S(1)}, u32[]{:S(2)}, u32[]{:S(2)}) collective-permute-start(bf16[64,512]{1,0:T(8,128)(2,1)S(1)} %copy-done.4), channel_id=1, source_target_pairs={{0,4},{4,8},{8,12},{1,5},{5,9},{9,13},{2,6},{6,10},{10,14},{3,7},{... | collective-permute-start | bytes 196616 | tf_op jit(solution)/shard_map/ppermute | solution.py:12
  55.6 0.1 iota_compare_fusion
  55.7 0.0 copy-done.3
  55.7 0.1 copy.15
  55.8 0.6 collective-permute-done.3
  56.4 1.1 collective-permute-done.2
  57.5 2.2 %all_gather.7 = bf16[3,64,1024]{2,1,0:T(8,128)(2,1)S(1)} all-gather(bf16[3,64,512]{2,1,0:T(8,128)(2,1)S(1)} %pad_maximum_fusion.1), channel_id=1, replica_groups=mesh['grp'=2,'seq'=4,'head'=2,'rep'=2] {'rep'}, dimensions={2}, use_global_device_ids=true | all-gather | bytes 589824 | tf_op jit(solution)/shard_map/all_gather | solution.py:59
  59.8 2.5 %all-gather.2.cloned.1.call-done = bf16[3,1024,512]{2,1,0:T(8,128)(2,1)} async-done(((bf16[3,512,512]{2,1,0:T(8,128)(2,1)}), bf16[3,1024,512]{2,1,0:T(8,128)(2,1)}) %all-gather.2.cloned.1.call-update) | async-done | bytes 3145744 | tf_op jit(solution)/shard_map/all_gather | solution.py:58
  62.2 0.0 copy-done
  62.2 2.6 %fusion.31 = f32[1024,128,8]{1,0,2:T(8,128)S(1)} fusion(bf16[3,1024,512]{2,1,0:T(8,128)(2,1)} %all-gather.2.cloned.1.call-done, bf16[128,8,512]{2,1,0:T(8,128)(2,1)S(1)} %copy-done), kind=kOutput, calls=%fused_computation.36 | convolution fusion | flops 1073741824 | bytes 6291456 | tf_op jit(solution)/shard_map/qhc,kc->hqk/dot_general | solution.py:27
  64.8 0.0 copy-start.2
  64.9 0.8 bitcast_reduce_fusion
  65.7 1.1 copy-done.2
  66.7 1.4 %fusion.30 = f32[1024,128,8]{1,0,2:T(8,128)S(1)} fusion(bf16[3,1024,512]{2,1,0:T(8,128)(2,1)S(1)} %copy-done.2, bf16[128,8,512]{2,1,0:T(8,128)(2,1)S(1)} %copy-done), kind=kOutput, calls=%fused_computation.35 | convolution fusion | flops 1073741824 | bytes 6291456 | tf_op jit(solution)/shard_map/qhc,kc->hqk/dot_general | solution.py:27
  68.2 0.8 bitcast_reduce_fusion.1
  69.0 1.4 %fusion.29 = f32[1024,128,8]{1,0,2:T(8,128)S(1)} fusion(bf16[3,1024,512]{2,1,0:T(8,128)(2,1)S(1)} %copy-done.2, bf16[128,8,512]{2,1,0:T(8,128)(2,1)S(1)} %copy-done), kind=kOutput, calls=%fused_computation.34 | convolution fusion | flops 1073741824 | bytes 6291456 | tf_op jit(solution)/shard_map/qhc,kc->hqk/dot_general | solution.py:27
  70.4 1.0 fusion.38
  71.4 0.0 copy-start.1
  71.4 0.6 fusion.6
  71.9 1.1 fusion.2
  73.1 0.2 copy-done.1
  73.3 1.3 %fusion.8 = f32[8,128,512]{2,1,0:T(8,128)S(1)} fusion(f32[1024,128,8]{1,0,2:T(8,128)S(1)} %get-tuple-element.13, f32[8,128]{1,0:T(8,128)S(1)} %get-tuple-element.8, bf16[3,1024,512]{2,1,0:T(8,128)(2,1)S(1)} %copy-done.2), kind=kOutput, calls=%fused_computation.17 | convolution fusion | flops 1075838976 | bytes 7344128 | tf_op jit(solution)/shard_map/hqk,kc->hqc/dot_general | solution.py:38
  74.6 2.7 %fusion.10 = f32[8,128,512]{2,1,0:T(8,128)} fusion(f32[1024,128,8]{1,0,2:T(8,128)S(1)} %get-tuple-element.15, f32[8,128]{1,0:T(8,128)S(1)} %get-tuple-element.9, bf16[3,1024,512]{2,1,0:T(8,128)(2,1)S(1)} %copy-done.2), kind=kOutput, calls=%fused_computation.18 | convolution fusion | flops 1075838976 | bytes 7344128 | tf_op jit(solution)/shard_map/hqk,kc->hqc/dot_general | solution.py:38
  77.3 5.4 %fusion.22 = bf16[8,128,128]{1,2,0:T(8,128)(2,1)S(1)} fusion(bf16[8,512,128]{2,1,0:T(8,128)(2,1)} %param.10, f32[8,128,512]{2,1,0:T(8,128)S(1)} %fusion.8, f32[8,128,512]{2,1,0:T(8,128)} %fusion.10, f32[8,128,1024]{1,2,0:T(8,128)} %copy-done.1, f32[8,128]{1,0:T(8,128)S(1)} %get-tuple-element.11, f32[8,128]{1,0:T(8,128)S(1)} %get-tuple-element.5, ...), kind=kOutput, calls=%fused_computation.26 | convolution fusion | flops 1213857792 | bytes 10768384 | tf_op jit(solution)/shard_map/hqc,hcv->qhv/dot_general | solution.py:82
  82.7 5.2 %convolution_convert_fusion = bf16[128,3584]{1,0:T(8,128)(2,1)} fusion(bf16[128,1024]{0,1:T(8,128)(2,1)S(1)} %bitcast.75, bf16[1024,3584]{1,0:T(8,128)(2,1)} %param.11), kind=kOutput, calls=%fused_computation | convolution fusion | flops 939982848 | bytes 8519680 | tf_op jit(solution)/shard_map/dot_general | solution.py:87
  87.8 0.0 reduce-scatter.2.cloned.1.call-update
  87.9 25.3 %reduce-scatter.2.cloned.1.call-done = bf16[32,3584]{1,0:T(8,128)(2,1)} async-done(((bf16[128,3584]{1,0:T(8,128)(2,1)}), bf16[32,3584]{1,0:T(8,128)(2,1)}) %reduce-scatter.2.cloned.1.call-update) | async-done | bytes 229392 | tf_op jit(solution)/shard_map/reduce_scatter | solution.py:86
  (4 shorter events, 0.1 us)
Async XLA Ops:
  6.5 55.7 %copy-start = (bf16[128,8,512]{2,1,0:T(8,128)(2,1)S(1)}, bf16[128,8,512]{2,1,0:T(8,128)(2,1)}, u32[]{:S(2)}) copy-start(bf16[128,8,512]{2,1,0:T(8,128)(2,1)} %param.6) | copy-start | bytes 3145732
  6.5 31.3 %copy-start.4 = (bf16[64,512]{1,0:T(8,128)(2,1)S(1)}, bf16[64,512]{1,0:T(8,128)(2,1)}, u32[]{:S(2)}) copy-start(bf16[64,512]{1,0:T(8,128)(2,1)} %param.9) | copy-start | bytes 196612
  6.5 49.2 %copy-start.3 = (bf16[128,512]{1,0:T(8,128)(2,1)S(1)}, bf16[128,512]{1,0:T(8,128)(2,1)}, u32[]{:S(2)}) copy-start(bf16[128,512]{1,0:T(8,128)(2,1)} %param.7) | copy-start | bytes 393220
  6.5 55.7 %all-gather.2.cloned.1.call-start = ((), (), s32[]{:S(2)}) async-start(), calls=%async_computation.1 | async-start | bytes 4718592 | tf_op jit(solution)/shard_map/all_gather | solution.py:58
  6.5 18.8 %collective-permute-start.1 = (bf16[512,512]{1,0:T(8,128)(2,1)}, bf16[512,512]{1,0:T(8,128)(2,1)S(1)}, u32[]{:S(2)}, u32[]{:S(2)}) collective-permute-start(bf16[512,512]{1,0:T(8,128)(2,1)} %param.8), channel_id=1, source_target_pairs={{0,8},{4,12},{1,9},{5,13},{2,10},{6,14},{3,11},{7,15},{16,24},{20,... | collective-permute-start | bytes 1572872 | tf_op jit(solution)/shard_map/ppermute | solution.py:12
  12.7 22.7 %collective-permute-start = (bf16[512,512]{1,0:T(8,128)(2,1)}, bf16[512,512]{1,0:T(8,128)(2,1)S(1)}, u32[]{:S(2)}, u32[]{:S(2)}) collective-permute-start(bf16[512,512]{1,0:T(8,128)(2,1)} %param.8), channel_id=1, source_target_pairs={{0,4},{4,8},{8,12},{1,5},{5,9},{9,13},{2,6},{6,10},{10,14},{3,7},{... | collective-permute-start | bytes 1572872 | tf_op jit(solution)/shard_map/ppermute | solution.py:12
  37.8 75.4 %reduce-scatter.2.cloned.1.call-start = ((), (), s32[]{:S(2)}) async-start(), calls=%async_computation.2 | async-start | bytes 1146880 | tf_op jit(solution)/shard_map/reduce_scatter | solution.py:86
  37.9 18.5 %collective-permute-start.3 = (bf16[64,512]{1,0:T(8,128)(2,1)S(1)}, bf16[64,512]{1,0:T(8,128)(2,1)S(1)}, u32[]{:S(2)}, u32[]{:S(2)}) collective-permute-start(bf16[64,512]{1,0:T(8,128)(2,1)S(1)} %copy-done.4), channel_id=1, source_target_pairs={{0,8},{4,12},{1,9},{5,13},{2,10},{6,14},{3,11},{7,15},{16,24},{20,... | collective-permute-start | bytes 196616 | tf_op jit(solution)/shard_map/ppermute | solution.py:12
  54.3 3.2 %collective-permute-start.2 = (bf16[64,512]{1,0:T(8,128)(2,1)S(1)}, bf16[64,512]{1,0:T(8,128)(2,1)S(1)}, u32[]{:S(2)}, u32[]{:S(2)}) collective-permute-start(bf16[64,512]{1,0:T(8,128)(2,1)S(1)} %copy-done.4), channel_id=1, source_target_pairs={{0,4},{4,8},{8,12},{1,5},{5,9},{9,13},{2,6},{6,10},{10,14},{3,7},{... | collective-permute-start | bytes 196616 | tf_op jit(solution)/shard_map/ppermute | solution.py:12
  64.8 1.9 %copy-start.2 = (bf16[3,1024,512]{2,1,0:T(8,128)(2,1)S(1)}, bf16[3,1024,512]{2,1,0:T(8,128)(2,1)}, u32[]{:S(2)}) copy-start(bf16[3,1024,512]{2,1,0:T(8,128)(2,1)} %all-gather.2.cloned.1.call-done) | copy-start | bytes 9437188
  71.4 1.9 %copy-start.1 = (f32[8,128,1024]{1,2,0:T(8,128)}, f32[8,128,1024]{1,2,0:T(8,128)S(1)}, u32[]{:S(2)}) copy-start(f32[8,128,1024]{1,2,0:T(8,128)S(1)} %get-tuple-element.17) | copy-start | bytes 12582916
Sparse Core Ops, SparseCore 0:
  37.9 24.2 all-gather.1
  88.0 25.1 reduce-scatter.1
where the time goes:
time: 120 us
  waiting for transfers between devices  48.7 us (41%)
  starting transfers between devices  27.4 us (23%)
  matrix products  22.5 us (19%)
  between operations  13.6 us (11%)
  other arithmetic  4.19 us (3%)
  blocking collectives  2.25 us (2%)
  local copies, waits for them, and re-layouts  1.43 us (1%)
    ppermute x4, starting transfers between devices, shifted(): return lax.ppermute(value, axis, pairs)  27.4 us
    reduce_scatter x1, waiting for transfers between devices, shards(): lax.psum_scatter(jnp.dot(expanded, out_proj, preferred_element_type=jnp.f...  25.3 us
    ppermute x4, waiting for transfers between devices, shifted(): return lax.ppermute(value, axis, pairs)  20.8 us
    dot_general x3, matrix products, attend_block(): jnp.einsum('qhc,kc->hqk', query_latent, block_latent, preferred_element_t...  5.41 us
    dot_general x1, matrix products, shards(): jnp.einsum('hqc,hcv->qhv', attended, value_up, preferred_element_type=jnp...  5.4 us
    dot_general x1, matrix products, shards(): jnp.dot(expanded, out_proj, preferred_element_type=jnp.float32)  5.16 us
    dot_general x2, matrix products, attend_block(): jnp.einsum('hqk,kc->hqc', weights.astype(jnp.bfloat16), block_latent, pre...  3.97 us
    dot_general x3, matrix products, attend_block(): jnp.einsum('qhr,rk->hqk', rope_queries, block_rope, preferred_element_typ...  2.57 us
  transfers between devices with their start and end apart: 6, of which 6 were waited for; matrix products, arithmetic and copies ran while one was open for 0% of the time, Pallas kernels for 0%

commit v1 on v0

v1 whole, which is shorter than its diff:
```python
import functools
import math

import jax
import jax.numpy as jnp
from jax import lax
from jax.experimental import pallas as pl
from jax.experimental.pallas import tpu as pltpu
from jax.sharding import PartitionSpec as P

masked_score = -1e30
lanes = 128
log2e = math.log2(math.e)
in_vmem = pl.BlockSpec(memory_space=pltpu.VMEM)
in_smem = pl.BlockSpec(memory_space=pltpu.SMEM)
anywhere = pl.BlockSpec(memory_space=pl.ANY)
contract_last = (((1,), (1,)), ((), ()))


def params(mib):
    return pltpu.CompilerParams(vmem_limit_bytes=mib << 20)


def shifted(value, axis, by):
    peers = lax.axis_size(axis)
    return lax.ppermute(value, axis, [(i, i + by) for i in range(peers) if 0 <= i + by < peers])


def rotated(value, axis, by):
    peers = lax.axis_size(axis)
    return lax.ppermute(value, axis, [(i, (i + by) % peers) for i in range(peers)])


def pack_kernel(part_ref, latent_ref, rope_ref, packed_ref, sems):
    width = latent_ref.shape[1]
    rope_width = rope_ref.shape[0]
    rows = packed_ref.shape[0] * width // (width + rope_width)
    folds = width // rows
    group = rope_width // folds
    start = pl.multiple_of(part_ref[0] * rows, rows)
    copies = [
        pltpu.make_async_copy(
            latent_ref.at[pl.ds(start, rows), :], packed_ref.at[pl.ds(0, rows), :], sems.at[0]
        )
    ]
    for fold in range(folds):
        copies.append(
            pltpu.make_async_copy(
                rope_ref.at[pl.ds(fold * group, group), pl.ds(start, rows)],
                packed_ref.at[pl.ds(rows, group), pl.ds(fold * rows, rows)],
                sems.at[fold + 1],
            )
        )
    for copy in copies:
        copy.start()
    for copy in copies:
        copy.wait()


def pack_part(part, parts, latent, key_rope):
    rows = latent.shape[0] // parts
    width = latent.shape[1]
    folds = width // rows
    group = key_rope.shape[0] // folds
    return pl.pallas_call(
        pack_kernel,
        out_shape=jax.ShapeDtypeStruct((rows + group, width), latent.dtype),
        in_specs=[in_smem, anywhere, anywhere],
        out_specs=in_vmem,
        scratch_shapes=[pltpu.SemaphoreType.DMA((folds + 1,))],
        compiler_params=params(4),
        cost_estimate=pl.CostEstimate(flops=0, bytes_accessed=600000, transcendentals=0),
        name="pack_part",
    )(part, latent, key_rope)


def read_piece(ref, rope_width):
    width = ref.shape[1]
    rows = ref.shape[0] * width // (width + rope_width)
    folds = width // rows
    group = rope_width // folds
    keys = ref[pl.ds(0, rows), :]
    ropes = [ref[pl.ds(rows, group), pl.ds(fold * rows, rows)] for fold in range(folds)]
    return keys, jnp.concatenate(ropes, axis=0)


def attend_rows(rows_here, query_ref, rope_ref, pieces, scale, state):
    query = query_ref[rows_here, :]
    rope = rope_ref[rows_here, :]
    scores = []
    for keys, ropes, mask, bias in pieces:
        score = lax.dot_general(query, keys, contract_last, preferred_element_type=jnp.float32)
        score = score + jnp.dot(rope, ropes, preferred_element_type=jnp.float32)
        if mask is not None:
            score = mask(score)
        scores.append(score)
    tops = []
    for score, (_, _, _, bias) in zip(scores, pieces):
        top = jnp.max(score, axis=1, keepdims=True) * scale
        tops.append(top if bias is None else top + bias)
    new_max = functools.reduce(jnp.maximum, tops)
    if state is not None:
        new_max = jnp.maximum(new_max, state[0])
    total = None
    out = None
    for score, (keys, _, _, bias) in zip(scores, pieces):
        shift = new_max if bias is None else new_max - bias
        weights = jnp.exp2(score * scale - shift)
        part = jnp.sum(weights, axis=1, keepdims=True)
        update = jnp.dot(weights.astype(keys.dtype), keys, preferred_element_type=jnp.float32)
        total = part if total is None else total + part
        out = update if out is None else out + update
    if state is not None:
        factor = jnp.exp2(state[0] - new_max)
        total = total + state[1] * factor
        out = out + state[2] * factor
    return new_max, total, out


def own_kernel(block, heads, scale, rep_ref, query_ref, qrope_ref, *refs):
    here_latent, here_rope, there_latent, there_rope, max_ref, sum_ref, out_ref = refs
    rows = query_ref.shape[0]
    half = here_latent.shape[0]
    queries = rows // heads

    for start in range(0, rows, block):
        rows_here = pl.ds(start, block)

        def causal(first, score):
            block_rows = 2 * half
            j = first + lax.broadcasted_iota(jnp.int32, score.shape, 1)
            q = (start + lax.broadcasted_iota(jnp.int32, score.shape, 0)) // heads
            return jnp.where(j <= block_rows - queries + q, score, masked_score)

        rep = rep_ref[0]
        pieces = [
            (here_latent[...], here_rope[...], functools.partial(causal, rep * half), None),
            (there_latent[...], there_rope[...], functools.partial(causal, (1 - rep) * half), None),
        ]
        state = attend_rows(rows_here, query_ref, qrope_ref, pieces, scale, None)
        max_ref[rows_here, :], sum_ref[rows_here, :], out_ref[rows_here, :] = state


def attention_cost(rows, keys, width):
    return pl.CostEstimate(
        flops=4 * rows * keys * width, bytes_accessed=2 * rows * width, transcendentals=rows * keys
    )


def attend_own(rep, query, query_rope, here, there, heads, scale):
    rows, width = query.shape
    out_shape = (
        jax.ShapeDtypeStruct((rows, 1), jnp.float32),
        jax.ShapeDtypeStruct((rows, 1), jnp.float32),
        jax.ShapeDtypeStruct((rows, width), jnp.float32),
    )
    return pl.pallas_call(
        functools.partial(own_kernel, math.gcd(rows, 256), heads, scale),
        out_shape=out_shape,
        in_specs=[in_smem] + [in_vmem] * 6,
        out_specs=[in_vmem] * 3,
        compiler_params=params(32),
        cost_estimate=attention_cost(rows, 2 * here[0].shape[0], width),
        name="attend_own",
    )(rep, query, query_rope, *here, *there)


def biased_pieces(levels_of, bias_ref, refs, rope_width):
    pieces = []
    for level, ref in zip(levels_of, refs):
        keys, ropes = read_piece(ref, rope_width)
        pieces.append((keys, ropes, None, bias_ref[level]))
    return pieces


def middle_kernel(block, levels_of, scale, bias_ref, query_ref, qrope_ref, *refs):
    count = len(levels_of)
    max_in, sum_in, out_in, max_ref, sum_ref, out_ref = refs[count:]
    rope_width = qrope_ref.shape[1]
    for start in range(0, query_ref.shape[0], block):
        rows_here = pl.ds(start, block)
        pieces = biased_pieces(levels_of, bias_ref, refs[:count], rope_width)
        state = (max_in[rows_here, :], sum_in[rows_here, :], out_in[rows_here, :])
        state = attend_rows(rows_here, query_ref, qrope_ref, pieces, scale, state)
        max_ref[rows_here, :], sum_ref[rows_here, :], out_ref[rows_here, :] = state


def attend_middle(bias, query, query_rope, pieces, levels_of, state, scale):
    rows, width = query.shape
    keys = sum(piece.shape[0] for piece in pieces)
    return pl.pallas_call(
        functools.partial(middle_kernel, math.gcd(rows, 256), tuple(levels_of), scale),
        out_shape=tuple(jax.ShapeDtypeStruct(s.shape, s.dtype) for s in state),
        in_specs=[in_smem] + [in_vmem] * (2 + len(pieces) + 3),
        out_specs=[in_vmem] * 3,
        compiler_params=params(32),
        cost_estimate=attention_cost(rows, keys, width),
        name="attend_middle",
    )(bias, query, query_rope, *pieces, *state)


def last_kernel(block, levels_of, heads, scale, peers, order_ref, bias_ref, query_ref, qrope_ref, *refs):
    count = len(levels_of)
    max_in, sum_in, out_in, up_ref, proj_ref, result_ref, norm_ref, exp_ref = refs[count:]
    rope_width = qrope_ref.shape[1]
    rows, width = query_ref.shape
    queries = rows // heads
    value = up_ref.shape[2]
    for start in range(0, rows, block):
        rows_here = pl.ds(start, block)
        pieces = biased_pieces(levels_of, bias_ref, refs[:count], rope_width)
        state = (max_in[rows_here, :], sum_in[rows_here, :], out_in[rows_here, :])
        _, total, out = attend_rows(rows_here, query_ref, qrope_ref, pieces, scale, state)
        norm = out * (1.0 / total)
        for tile in range(width // lanes):
            norm_ref[tile, rows_here, :] = norm[:, tile * lanes : (tile + 1) * lanes]
    for head in range(heads):
        tiles = [
            norm_ref[tile, pl.ds(head, queries, stride=heads), :].astype(jnp.bfloat16)
            for tile in range(width // lanes)
        ]
        attended = jnp.concatenate(tiles, axis=1)
        expanded = jnp.dot(attended, up_ref[head], preferred_element_type=jnp.float32)
        exp_ref[:, pl.ds(head * value, value)] = expanded.astype(jnp.bfloat16)
    chunk = queries // peers
    parts = [exp_ref[pl.ds(pl.multiple_of(order_ref[i] * chunk, chunk), chunk), :] for i in range(peers)]
    lhs = jnp.concatenate(parts, axis=0)
    columns = proj_ref.shape[1]
    step = math.gcd(columns, 512)
    for column in range(0, columns, step):
        piece = jnp.dot(lhs, proj_ref[:, pl.ds(column, step)], preferred_element_type=jnp.float32)
        result_ref[:, pl.ds(column, step)] = piece.astype(result_ref.dtype)


def attend_last(order, bias, query, query_rope, pieces, levels_of, state, scale, value_up, out_proj):
    rows, width = query.shape
    heads = value_up.shape[0]
    queries = rows // heads
    keys = sum(piece.shape[0] for piece in pieces)
    columns = out_proj.shape[1]
    return pl.pallas_call(
        functools.partial(
            last_kernel, math.gcd(rows, 256), tuple(levels_of), heads, scale, order.shape[0]
        ),
        out_shape=jax.ShapeDtypeStruct((queries, columns), jnp.bfloat16),
        in_specs=[in_smem, in_smem] + [in_vmem] * (2 + len(pieces) + 3 + 2),
        out_specs=in_vmem,
        scratch_shapes=[
            pltpu.VMEM((width // lanes, rows, lanes), jnp.float32),
            pltpu.VMEM((queries, out_proj.shape[0]), jnp.bfloat16),
        ],
        compiler_params=params(40),
        cost_estimate=attention_cost(rows, keys, width),
        name="attend_last",
    )(order, bias, query, query_rope, *pieces, *state, value_up, out_proj)


def shards(query_latent, query_rope, latent, key_rope, value_up, out_proj):
    queries, heads, width = query_latent.shape
    rope_width = key_rope.shape[0]
    levels = min(4, lax.axis_size("seq") // 4 + 1)
    columns = lax.axis_size("head")
    column = lax.axis_index("head")
    rep = lax.axis_index("rep")
    shard_index = lax.axis_index("seq")
    scale = (width + rope_width) ** (-0.5) * log2e
    bias = jnp.stack(
        [jnp.where(shard_index >= 2**level, 0.0, masked_score) for level in range(levels)]
    ).astype(jnp.float32)
    query = query_latent.reshape(queries * heads, width)
    qrope = query_rope.reshape(queries * heads, rope_width)

    part = pack_part(column[None], columns, latent, key_rope)
    by_level = []
    moved = part
    for level in range(levels):
        moved = shifted(moved, "seq", 1 if level == 0 else 2 ** (level - 1))
        by_level.append(moved)
    there = (rotated(latent, "rep", 1), rotated(key_rope, "rep", 1))
    state = attend_own(rep[None], query, qrope, (latent, key_rope), there, heads, scale)

    middle, middle_levels, last, last_levels = [], [], [], []
    for level in range(levels):
        direct = by_level[level]
        crossed = [rotated(direct, "head", by) for by in range(1, columns)]
        for index, piece in enumerate([direct] + crossed):
            both = [piece, rotated(piece, "rep", 1)]
            if level == levels - 1 and index > 0:
                last += both
                last_levels += [level] * 2
            else:
                middle += both
                middle_levels += [level] * 2
    state = attend_middle(bias, query, qrope, middle, middle_levels, state, scale)

    chips = [(column + by) % columns for by in range(1, columns + 1)]
    order = jnp.stack([chip * 2 + 1 - rep for chip in chips] + [chip * 2 + rep for chip in chips])
    partial = attend_last(
        order, bias, query, qrope, last, last_levels, state, scale, value_up, out_proj
    )
    half = queries // 2
    arrived = rotated(partial[:half], "rep", 1)
    chunk = half // columns
    kept = partial[half:]
    sums = []
    for index in range(columns):
        rows = slice(index * chunk, (index + 1) * chunk)
        sums.append(kept[rows].astype(jnp.float32) + arrived[rows].astype(jnp.float32))
    result = sums[-1]
    for index in range(columns - 1):
        result = result + rotated(sums[index].astype(jnp.bfloat16), "head", index + 1).astype(
            jnp.float32
        )
    return result.astype(jnp.bfloat16)


def solution(mesh):
    placed = (
        P(("grp", "seq"), ("head", "rep"), None),
        P(("grp", "seq"), ("head", "rep")),
        P(("grp", "seq", "rep"), None),
        P(None, ("grp", "seq", "rep")),
        P(("head", "rep"), None, None),
        P(("head", "rep"), None),
    )
    return jax.shard_map(
        shards,
        mesh=mesh,
        in_specs=placed,
        out_specs=P(("grp", "seq", "head", "rep"), None),
        check_vma=False,
    )
```

time: 120 us -> 54.1 us (0.45)
  waiting for transfers between devices: 48.7 us -> 17.8 us
  matrix products: 22.5 us -> 0 us
  Pallas kernels: 0 us -> 17.3 us
  between operations: 13.6 us -> 0.17 us
  starting transfers between devices: 27.4 us -> 15.1 us
  other arithmetic: 4.19 us -> 0.98 us
  blocking collectives: 2.25 us -> 0 us
    reduce_scatter x1 -> x0, waiting for transfers between devices: 25.3 us -> none  [shards(): lax.psum_scatter(jnp.dot(expanded, out_proj, preferred_element_type=jnp.f...]
    dot_general x10 -> x0, matrix products: 22.5 us -> none  [the longest x3 5.41 us: attend_block(): jnp.einsum('qhc,kc->hqk', query_latent, block_latent, preferred_element_t...]
    pallas_call x0 -> x4, Pallas kernels: none -> 17.3 us  [the longest x1 6.4 us: attend_middle(): pl.pallas_call(functools.partial(middle_kernel, math.gcd(rows, 256), tupl...]
    ppermute x4 -> x12, starting transfers between devices: 27.4 us -> 15.1 us  [the longest x2 9.37 us: shifted(): lax.ppermute(value, axis, [(i, i + by) for i in range(peers) if 0 <= i +...]
    ppermute x4 -> x12, waiting for transfers between devices: 20.8 us -> 17.8 us  [the longest x10 9.57 us: rotated(): lax.ppermute(value, axis, [(i, (i + by) % peers) for i in range(peers)])]
    all_gather x1 -> x0, waiting for transfers between devices: 2.48 us -> none  [shards(): lax.all_gather(stacked_latent, 'rep', axis=1, tiled=True)]
    all_gather x1 -> x0, blocking collectives: 2.25 us -> none  [shards(): lax.all_gather(stacked_rope, 'rep', axis=2, tiled=True)]
    another operation x2, other arithmetic: 2.39 us -> 0.15 us  [the longest x1 0.08 us: shards(): jnp.stack([chip * 2 + 1 - rep for chip in chips] + [chip * 2 + rep for ch...]
  transfers between devices with their start and end apart: 6 -> 12, of which waited for: 6 -> 6; matrix products, arithmetic and copies ran while one was open for 0% -> 2% of each run, Pallas kernels for 0% -> 21%
where the time goes in v1:
time: 54.1 us; the launch traced here: 53.8 us
  waiting for transfers between devices  17.8 us (33%)
  Pallas kernels  17.3 us (32%)
  starting transfers between devices  15.1 us (28%)
  local copies, waits for them, and re-layouts  2.38 us (4%)
  other arithmetic  0.98 us (2%)
    ppermute x10, waiting for transfers between devices, rotated(): lax.ppermute(value, axis, [(i, (i + by) % peers) for i in range(peers)])  9.57 us
    ppermute x2, starting transfers between devices, shifted(): lax.ppermute(value, axis, [(i, i + by) for i in range(peers) if 0 <= i +...  9.37 us
    ppermute x2, waiting for transfers between devices, shifted(): lax.ppermute(value, axis, [(i, i + by) for i in range(peers) if 0 <= i +...  8.26 us
    pallas_call x1, Pallas kernels, attend_middle(): pl.pallas_call(functools.partial(middle_kernel, math.gcd(rows, 256), tupl...  6.4 us
    ppermute x10, starting transfers between devices, rotated(): lax.ppermute(value, axis, [(i, (i + by) % peers) for i in range(peers)])  5.77 us
    pallas_call x1, Pallas kernels, attend_last(): pl.pallas_call(functools.partial(last_kernel, math.gcd(rows, 256), tuple(...  5.07 us
    pallas_call x1, Pallas kernels, attend_own(): pl.pallas_call(functools.partial(own_kernel, math.gcd(rows, 256), heads,...  4.87 us
    unnamed x10, local copies, waits for them, and re-layouts  1.25 us
  transfers between devices with their start and end apart: 12, of which 6 were waited for; matrix products, arithmetic and copies ran while one was open for 2% of the time, Pallas kernels for 21%

profile of v1, /device:TPU:0, one launch (start us, length us, event | category | flops | bytes accessed | tf_op | source)
XLA Modules:
  0.0 53.8 jit_solution(12406043592804580965)
XLA Ops:
  0.0 1.0 %pack_part.1 = bf16[288,512]{1,0:T(8,128)(2,1)S(1)} custom-call(s32[1]{0:T(128)} %bitcast.7.part_ref, bf16[512,512]{1,0:T(8,128)(2,1)} %refs_0_.1, bf16[64,512]{1,0:T(8,128)(2,1)} %refs_1_.1), custom_call_target="tpu_custom_call" | custom-call | bytes 600000 | tf_op jit(solution)/shard_map/pack_part/pallas_call | solution.py:65
  1.0 5.0 %collective-permute-start = (bf16[288,512]{1,0:T(8,128)(2,1)S(1)}, bf16[288,512]{1,0:T(8,128)(2,1)S(1)}, u32[]{:S(2)}, u32[]{:S(2)}) collective-permute-start(bf16[288,512]{1,0:T(8,128)(2,1)S(1)} %pack_part.1), channel_id=1, source_target_pairs={{0,4},{4,8},{8,12},{1,5},{5,9},{9,13},{2,6},{6,10},{10,14},{3,7},{... | collective-permute-start | bytes 884744 | tf_op jit(solution)/shard_map/ppermute | solution.py:26
  6.0 0.1 collective-permute-start.8
  6.0 6.1 %collective-permute-done.refs_0_ = bf16[288,512]{1,0:T(8,128)(2,1)S(1)} collective-permute-done((bf16[288,512]{1,0:T(8,128)(2,1)S(1)}, bf16[288,512]{1,0:T(8,128)(2,1)S(1)}, u32[]{:S(2)}, u32[]{:S(2)}) %collective-permute-start) | collective-permute-done | bytes 294944 | tf_op jit(solution)/shard_map/ppermute | solution.py:26
  12.2 4.4 %collective-permute-start.1 = (bf16[288,512]{1,0:T(8,128)(2,1)S(1)}, bf16[288,512]{1,0:T(8,128)(2,1)S(1)}, u32[]{:S(2)}, u32[]{:S(2)}) collective-permute-start(bf16[288,512]{1,0:T(8,128)(2,1)S(1)} %collective-permute-done.refs_0_), channel_id=1, source_target_pairs={{0,4},{4,8},{8,12},{1,5},{5,9},{9,13},{2,6},{6,10},{10,14},{3,7},{... | collective-permute-start | bytes 884744 | tf_op jit(solution)/shard_map/ppermute | solution.py:26
  16.6 1.6 %collective-permute-start.5 = (bf16[288,512]{1,0:T(8,128)(2,1)S(1)}, bf16[288,512]{1,0:T(8,128)(2,1)S(1)}, u32[]{:S(2)}, u32[]{:S(2)}) collective-permute-start(bf16[288,512]{1,0:T(8,128)(2,1)S(1)} %collective-permute-done.refs_0_), channel_id=1, source_target_pairs={{0,2},{2,0},{1,3},{3,1},{4,6},{6,4},{5,7},{7,5},{8,10},{10,8},{9,1... | collective-permute-start | bytes 884744 | tf_op jit(solution)/shard_map/ppermute | solution.py:31
  18.2 0.0 collective-permute-start.9
  18.2 1.1 %reshape.7.qrope_ref = bf16[1024,64]{1,0:T(8,128)(2,1)S(1)} reshape(bf16[128,512]{1,0:T(8,128)(2,1)} %param.7) | data formatting | bytes 262144 | tf_op jit(solution)/shard_map/reshape | solution.py:271
  19.3 0.1 pad_maximum_fusion.bias_ref
  19.4 0.5 collective-permute-start.4
  19.9 2.1 %collective-permute-done.1.refs_4_ = bf16[288,512]{1,0:T(8,128)(2,1)S(1)} collective-permute-done((bf16[288,512]{1,0:T(8,128)(2,1)S(1)}, bf16[288,512]{1,0:T(8,128)(2,1)S(1)}, u32[]{:S(2)}, u32[]{:S(2)}) %collective-permute-start.1) | collective-permute-done | bytes 294944 | tf_op jit(solution)/shard_map/ppermute | solution.py:26
  22.0 0.0 collective-permute-start.7
  22.0 0.0 collective-permute-done.9.refs_3_
  22.0 1.5 %collective-permute-start.2 = (bf16[288,512]{1,0:T(8,128)(2,1)S(1)}, bf16[288,512]{1,0:T(8,128)(2,1)S(1)}, u32[]{:S(2)}, u32[]{:S(2)}) collective-permute-start(bf16[288,512]{1,0:T(8,128)(2,1)S(1)} %collective-permute-done.1.refs_4_), channel_id=1, source_target_pairs={{0,2},{2,0},{1,3},{3,1},{4,6},{6,4},{5,7},{7,5},{8,10},{10,8},{9,1... | collective-permute-start | bytes 884744 | tf_op jit(solution)/shard_map/ppermute | solution.py:31
  23.5 0.8 %collective-permute-done.5.refs_2_ = bf16[288,512]{1,0:T(8,128)(2,1)S(1)} collective-permute-done((bf16[288,512]{1,0:T(8,128)(2,1)S(1)}, bf16[288,512]{1,0:T(8,128)(2,1)S(1)}, u32[]{:S(2)}, u32[]{:S(2)}) %collective-permute-start.5) | collective-permute-done | bytes 294944 | tf_op jit(solution)/shard_map/ppermute | solution.py:31
  24.3 0.0 collective-permute-start.6
  24.3 0.1 pad_add_fusion.order_ref
  24.4 0.0 collective-permute-done.8.refs_2_
  24.4 0.0 copy-start
  24.4 1.2 %copy-done = bf16[128,8,512]{2,1,0:T(8,128)(2,1)S(1)} copy-done((bf16[128,8,512]{2,1,0:T(8,128)(2,1)S(1)}, bf16[128,8,512]{2,1,0:T(8,128)(2,1)}, u32[]{:S(2)}) %copy-start) | copy-done | bytes 1048600
  25.6 0.0 copy-start.1
  25.6 4.9 %attend_own.1 = (f32[1024,1]{1,0:T(8,128)S(1)}, f32[1024,1]{1,0:T(8,128)S(1)}, f32[1024,512]{1,0:T(8,128)S(1)}) custom-call(s32[1]{0:T(128)} %bitcast.8.rep_ref, bf16[1024,512]{1,0:T(8,128)(2,1)S(1)} %bitcast.11, bf16[1024,64]{1,0:T(8,128)(2,1)S(1)} %reshape.7.qrope_ref, bf16[512,512]{1,0:T(8,128)(2,1)} %refs_0_.1, bf16[64,512]{1,0:T(8,128)(2,1)} %refs_1_.1, ...), custom_call_target="tpu_custom_call" | custom-call | flops 2147483648 | bytes 1048576 | tf_op jit(solution)/shard_map/attend_own/pallas_call | solution.py:157
  30.5 0.9 %collective-permute-done.2.refs_0_ = bf16[288,512]{1,0:T(8,128)(2,1)S(1)} collective-permute-done((bf16[288,512]{1,0:T(8,128)(2,1)S(1)}, bf16[288,512]{1,0:T(8,128)(2,1)S(1)}, u32[]{:S(2)}, u32[]{:S(2)}) %collective-permute-start.2) | collective-permute-done | bytes 294944 | tf_op jit(solution)/shard_map/ppermute | solution.py:31
  31.4 0.0 collective-permute-start.3
  31.4 0.0 collective-permute-done.4.refs_1_
  31.4 0.0 collective-permute-done.7.refs_5_
  31.4 0.0 collective-permute-done.6.refs_3_
  31.4 0.0 slice-start
  31.4 0.0 copy-done.1
  31.4 0.0 slice-start.1
  31.5 0.0 copy-start.2
  31.5 6.4 %attend_middle.1 = (f32[1024,1]{1,0:T(8,128)S(1)}, f32[1024,1]{1,0:T(8,128)S(1)}, f32[1024,512]{1,0:T(8,128)S(1)}) custom-call(f32[2]{0:T(128)S(1)} %pad_maximum_fusion.bias_ref, bf16[1024,512]{1,0:T(8,128)(2,1)S(1)} %bitcast.12, bf16[1024,64]{1,0:T(8,128)(2,1)S(1)} %reshape.7.qrope_ref, bf16[288,512]{1,0:T(8,128)(2,1)S(1)} %collective-permute-done.refs_0_, ...), custom_call_target="tpu_custom_call" | custom-call | flops 3623878656 | bytes 1048576 | tf_op jit(solution)/shard_map/attend_middle/pallas_call | solution.py:191
  37.9 0.0 collective-permute-done.3.refs_1_
  37.9 0.0 slice-done
  37.9 0.0 slice-done.1
  37.9 0.0 copy-done.2
  37.9 5.1 %attend_last.1 = bf16[128,3584]{1,0:T(8,128)(2,1)S(1)} custom-call(s32[4]{0:T(128)S(1)} %pad_add_fusion.order_ref, f32[2]{0:T(128)S(1)} %pad_maximum_fusion.bias_ref, bf16[1024,512]{1,0:T(8,128)(2,1)S(1)} %bitcast.13, bf16[1024,64]{1,0:T(8,128)(2,1)S(1)} %reshape.7.qrope_ref, bf16[288,512]{1,0:T(8,128)(2,1)S(1)} %collective-permute-done.2.refs_0_, ...), custom_call_target="tpu_custom_call" | custom-call | flops 1207959552 | bytes 1048576 | tf_op jit(solution)/shard_map/attend_last/pallas_call | solution.py:241
  43.1 0.6 %collective-permute-start.10 = (bf16[64,3584]{1,0:T(8,128)(2,1)S(1)}, bf16[64,3584]{1,0:T(8,128)(2,1)S(1)}, u32[]{:S(2)}, u32[]{:S(2)}) collective-permute-start(bf16[64,3584]{1,0:T(8,128)(2,1)S(1)} %slice.24), channel_id=1, source_target_pairs={{0,1},{1,0},{2,3},{3,2},{4,5},{5,4},{6,7},{7,6},{8,9},{9,8},{10,11... | collective-permute-start | bytes 1376264 | tf_op jit(solution)/shard_map/ppermute | solution.py:31
  43.6 1.4 %collective-permute-done.10 = bf16[64,3584]{1,0:T(8,128)(2,1)S(1)} collective-permute-done((bf16[64,3584]{1,0:T(8,128)(2,1)S(1)}, bf16[64,3584]{1,0:T(8,128)(2,1)S(1)}, u32[]{:S(2)}, u32[]{:S(2)}) %collective-permute-start.10) | collective-permute-done | bytes 458784 | tf_op jit(solution)/shard_map/ppermute | solution.py:31
  45.0 0.1 add_convert_fusion.1
  45.1 1.6 %collective-permute-start.11 = (bf16[32,3584]{1,0:T(8,128)(2,1)S(1)}, bf16[32,3584]{1,0:T(8,128)(2,1)S(1)}, u32[]{:S(2)}, u32[]{:S(2)}) collective-permute-start(bf16[32,3584]{1,0:T(8,128)(2,1)S(1)} %add_convert_fusion.1), channel_id=1, source_target_pairs={{0,2},{2,0},{1,3},{3,1},{4,6},{6,4},{5,7},{7,5},{8,10},{10,8},{9,1... | collective-permute-start | bytes 688136 | tf_op jit(solution)/shard_map/ppermute | solution.py:31
  46.7 6.4 %collective-permute-done.11 = bf16[32,3584]{1,0:T(8,128)(2,1)S(1)} collective-permute-done((bf16[32,3584]{1,0:T(8,128)(2,1)S(1)}, bf16[32,3584]{1,0:T(8,128)(2,1)S(1)}, u32[]{:S(2)}, u32[]{:S(2)}) %collective-permute-start.11) | collective-permute-done | bytes 229408 | tf_op jit(solution)/shard_map/ppermute | solution.py:31
  53.1 0.8 %add_convert_fusion = bf16[32,3584]{1,0:T(8,128)(2,1)} fusion(bf16[32,3584]{1,0:T(8,128)(2,1)S(1)} %collective-permute-done.11, bf16[64,3584]{1,0:T(8,128)(2,1)S(1)} %collective-permute-done.10, bf16[128,3584]{1,0:T(8,128)(2,1)S(1)} %attend_last.1), kind=kLoop, calls=%fused_computation | loop fusion | flops 688128 | bytes 917504 | tf_op jit(solution)/shard_map/convert_element_type | solution.py:314
  (2 shorter events, 0.0 us)
Async XLA Ops:
  1.0 11.2 %collective-permute-start = (bf16[288,512]{1,0:T(8,128)(2,1)S(1)}, bf16[288,512]{1,0:T(8,128)(2,1)S(1)}, u32[]{:S(2)}, u32[]{:S(2)}) collective-permute-start(bf16[288,512]{1,0:T(8,128)(2,1)S(1)} %pack_part.1), channel_id=1, source_target_pairs={{0,4},{4,8},{8,12},{1,5},{5,9},{9,13},{2,6},{6,10},{10,14},{3,7},{... | collective-permute-start | bytes 884744 | tf_op jit(solution)/shard_map/ppermute | solution.py:26
  6.0 18.4 %collective-permute-start.8 = (bf16[512,512]{1,0:T(8,128)(2,1)}, bf16[512,512]{1,0:T(8,128)(2,1)S(1)}, u32[]{:S(2)}, u32[]{:S(2)}) collective-permute-start(bf16[512,512]{1,0:T(8,128)(2,1)} %refs_0_.1), channel_id=1, source_target_pairs={{0,1},{1,0},{2,3},{3,2},{4,5},{5,4},{6,7},{7,6},{8,9},{9,8},{10,11... | collective-permute-start | bytes 1572872 | tf_op jit(solution)/shard_map/ppermute | solution.py:31
  12.2 9.8 %collective-permute-start.1 = (bf16[288,512]{1,0:T(8,128)(2,1)S(1)}, bf16[288,512]{1,0:T(8,128)(2,1)S(1)}, u32[]{:S(2)}, u32[]{:S(2)}) collective-permute-start(bf16[288,512]{1,0:T(8,128)(2,1)S(1)} %collective-permute-done.refs_0_), channel_id=1, source_target_pairs={{0,4},{4,8},{8,12},{1,5},{5,9},{9,13},{2,6},{6,10},{10,14},{3,7},{... | collective-permute-start | bytes 884744 | tf_op jit(solution)/shard_map/ppermute | solution.py:26
  16.6 7.7 %collective-permute-start.5 = (bf16[288,512]{1,0:T(8,128)(2,1)S(1)}, bf16[288,512]{1,0:T(8,128)(2,1)S(1)}, u32[]{:S(2)}, u32[]{:S(2)}) collective-permute-start(bf16[288,512]{1,0:T(8,128)(2,1)S(1)} %collective-permute-done.refs_0_), channel_id=1, source_target_pairs={{0,2},{2,0},{1,3},{3,1},{4,6},{6,4},{5,7},{7,5},{8,10},{10,8},{9,1... | collective-permute-start | bytes 884744 | tf_op jit(solution)/shard_map/ppermute | solution.py:31
  18.2 3.8 %collective-permute-start.9 = (bf16[64,512]{1,0:T(8,128)(2,1)}, bf16[64,512]{1,0:T(8,128)(2,1)S(1)}, u32[]{:S(2)}, u32[]{:S(2)}) collective-permute-start(bf16[64,512]{1,0:T(8,128)(2,1)} %refs_1_.1), channel_id=1, source_target_pairs={{0,1},{1,0},{2,3},{3,2},{4,5},{5,4},{6,7},{7,6},{8,9},{9,8},{10,11... | collective-permute-start | bytes 196616 | tf_op jit(solution)/shard_map/ppermute | solution.py:31
  19.4 12.1 %collective-permute-start.4 = (bf16[288,512]{1,0:T(8,128)(2,1)S(1)}, bf16[288,512]{1,0:T(8,128)(2,1)S(1)}, u32[]{:S(2)}, u32[]{:S(2)}) collective-permute-start(bf16[288,512]{1,0:T(8,128)(2,1)S(1)} %collective-permute-done.refs_0_), channel_id=1, source_target_pairs={{0,1},{1,0},{2,3},{3,2},{4,5},{5,4},{6,7},{7,6},{8,9},{9,8},{10,11... | collective-permute-start | bytes 884744 | tf_op jit(solution)/shard_map/ppermute | solution.py:31
  22.0 9.4 %collective-permute-start.7 = (bf16[288,512]{1,0:T(8,128)(2,1)S(1)}, bf16[288,512]{1,0:T(8,128)(2,1)S(1)}, u32[]{:S(2)}, u32[]{:S(2)}) collective-permute-start(bf16[288,512]{1,0:T(8,128)(2,1)S(1)} %collective-permute-done.1.refs_4_), channel_id=1, source_target_pairs={{0,1},{1,0},{2,3},{3,2},{4,5},{5,4},{6,7},{7,6},{8,9},{9,8},{10,11... | collective-permute-start | bytes 884744 | tf_op jit(solution)/shard_map/ppermute | solution.py:31
  22.0 9.4 %collective-permute-start.2 = (bf16[288,512]{1,0:T(8,128)(2,1)S(1)}, bf16[288,512]{1,0:T(8,128)(2,1)S(1)}, u32[]{:S(2)}, u32[]{:S(2)}) collective-permute-start(bf16[288,512]{1,0:T(8,128)(2,1)S(1)} %collective-permute-done.1.refs_4_), channel_id=1, source_target_pairs={{0,2},{2,0},{1,3},{3,1},{4,6},{6,4},{5,7},{7,5},{8,10},{10,8},{9,1... | collective-permute-start | bytes 884744 | tf_op jit(solution)/shard_map/ppermute | solution.py:31
  24.3 7.1 %collective-permute-start.6 = (bf16[288,512]{1,0:T(8,128)(2,1)S(1)}, bf16[288,512]{1,0:T(8,128)(2,1)S(1)}, u32[]{:S(2)}, u32[]{:S(2)}) collective-permute-start(bf16[288,512]{1,0:T(8,128)(2,1)S(1)} %collective-permute-done.5.refs_2_), channel_id=1, source_target_pairs={{0,1},{1,0},{2,3},{3,2},{4,5},{5,4},{6,7},{7,6},{8,9},{9,8},{10,11... | collective-permute-start | bytes 884744 | tf_op jit(solution)/shard_map/ppermute | solution.py:31
  24.4 1.2 %copy-start = (bf16[128,8,512]{2,1,0:T(8,128)(2,1)S(1)}, bf16[128,8,512]{2,1,0:T(8,128)(2,1)}, u32[]{:S(2)}) copy-start(bf16[128,8,512]{2,1,0:T(8,128)(2,1)} %param.6) | copy-start | bytes 3145732
  25.6 5.9 %copy-start.1 = (bf16[128,8,512]{2,1,0:T(8,128)(2,1)S(1)}, bf16[128,8,512]{2,1,0:T(8,128)(2,1)}, u32[]{:S(2)}) copy-start(bf16[128,8,512]{2,1,0:T(8,128)(2,1)} %param.6) | copy-start | bytes 3145732
  31.4 6.5 %collective-permute-start.3 = (bf16[288,512]{1,0:T(8,128)(2,1)S(1)}, bf16[288,512]{1,0:T(8,128)(2,1)S(1)}, u32[]{:S(2)}, u32[]{:S(2)}) collective-permute-start(bf16[288,512]{1,0:T(8,128)(2,1)S(1)} %collective-permute-done.2.refs_0_), channel_id=1, source_target_pairs={{0,1},{1,0},{2,3},{3,2},{4,5},{5,4},{6,7},{7,6},{8,9},{9,8},{10,11... | collective-permute-start | bytes 884744 | tf_op jit(solution)/shard_map/ppermute | solution.py:31
  31.4 6.5 %slice-start = ((s8[7340032]{0:T(1024)(128)(4,1)}), s8[4194304]{0:T(1024)(128)(4,1)S(1)}, s32[]{:S(2)}) async-start(s8[7340032]{0:T(1024)(128)(4,1)} %bitcast.9), calls=%async_computation | async-start | bytes 8388608
  31.4 6.5 %slice-start.1 = ((s8[7340032]{0:T(1024)(128)(4,1)}), s8[3145728]{0:T(1024)(128)(4,1)S(1)}, s32[]{:S(2)}) async-start(s8[7340032]{0:T(1024)(128)(4,1)} %bitcast.9), calls=%async_computation.1 | async-start | bytes 6291456
  31.5 6.5 %copy-start.2 = (bf16[8,512,128]{2,1,0:T(8,128)(2,1)S(1)}, bf16[8,512,128]{2,1,0:T(8,128)(2,1)}, u32[]{:S(2)}) copy-start(bf16[8,512,128]{2,1,0:T(8,128)(2,1)} %refs_5_.1) | copy-start | bytes 3145732
  43.1 2.0 %collective-permute-start.10 = (bf16[64,3584]{1,0:T(8,128)(2,1)S(1)}, bf16[64,3584]{1,0:T(8,128)(2,1)S(1)}, u32[]{:S(2)}, u32[]{:S(2)}) collective-permute-start(bf16[64,3584]{1,0:T(8,128)(2,1)S(1)} %slice.24), channel_id=1, source_target_pairs={{0,1},{1,0},{2,3},{3,2},{4,5},{5,4},{6,7},{7,6},{8,9},{9,8},{10,11... | collective-permute-start | bytes 1376264 | tf_op jit(solution)/shard_map/ppermute | solution.py:31
  45.1 7.9 %collective-permute-start.11 = (bf16[32,3584]{1,0:T(8,128)(2,1)S(1)}, bf16[32,3584]{1,0:T(8,128)(2,1)S(1)}, u32[]{:S(2)}, u32[]{:S(2)}) collective-permute-start(bf16[32,3584]{1,0:T(8,128)(2,1)S(1)} %add_convert_fusion.1), channel_id=1, source_target_pairs={{0,2},{2,0},{1,3},{3,1},{4,6},{6,4},{5,7},{7,5},{8,10},{10,8},{9,1... | collective-permute-start | bytes 688136 | tf_op jit(solution)/shard_map/ppermute | solution.py:31

commit v2 on v1

--- a/solution.py
+++ b/solution.py
@@ -8,22 +8,27 @@
 from jax.experimental.pallas import tpu as pltpu
 from jax.sharding import PartitionSpec as P
 
+
 masked_score = -1e30
 lanes = 128
 log2e = math.log2(math.e)
 in_vmem = pl.BlockSpec(memory_space=pltpu.VMEM)
 in_smem = pl.BlockSpec(memory_space=pltpu.SMEM)
-anywhere = pl.BlockSpec(memory_space=pl.ANY)
+in_hbm = pl.BlockSpec(memory_space=pltpu.HBM)
 contract_last = (((1,), (1,)), ((), ()))
+
+
+def kept_in_hbm(value):
+    return pltpu.with_memory_space_constraint(value, pltpu.HBM)
 
 
 def params(mib):
     return pltpu.CompilerParams(vmem_limit_bytes=mib << 20)
 
 
-def shifted(value, axis, by):
+def shifted(value, axis, by, first):
     peers = lax.axis_size(axis)
-    return lax.ppermute(value, axis, [(i, i + by) for i in range(peers) if 0 <= i + by < peers])
+    return lax.ppermute(value, axis, [(i, i + by) for i in range(first, peers - by)])
 
 
 def rotated(value, axis, by):
@@ -65,13 +70,13 @@
     return pl.pallas_call(
         pack_kernel,
         out_shape=jax.ShapeDtypeStruct((rows + group, width), latent.dtype),
-        in_specs=[in_smem, anywhere, anywhere],
+        in_specs=[in_smem, in_hbm, in_hbm],
         out_specs=in_vmem,
         scratch_shapes=[pltpu.SemaphoreType.DMA((folds + 1,))],
         compiler_params=params(4),
         cost_estimate=pl.CostEstimate(flops=0, bytes_accessed=600000, transcendentals=0),
         name="pack_part",
-    )(part, latent, key_rope)
+    )(part, kept_in_hbm(latent), kept_in_hbm(key_rope))
 
 
 def read_piece(ref, rope_width):
@@ -117,24 +122,32 @@
     return new_max, total, out
 
 
-def own_kernel(block, heads, scale, rep_ref, query_ref, qrope_ref, *refs):
-    here_latent, here_rope, there_latent, there_rope, max_ref, sum_ref, out_ref = refs
+def own_kernel(block, heads, scale, rep_ref, query_hbm, qrope_ref, latent_hbm, rope_hbm, *refs):
+    there_latent, there_rope, query_ref, max_ref, sum_ref, out_ref, latent_ref, rope_ref, sems = refs
+    copies = [
+        pltpu.make_async_copy(query_hbm, query_ref, sems.at[0]),
+        pltpu.make_async_copy(latent_hbm, latent_ref, sems.at[1]),
+        pltpu.make_async_copy(rope_hbm, rope_ref, sems.at[2]),
+    ]
+    for copy in copies:
+        copy.start()
+    for copy in copies:
+        copy.wait()
     rows = query_ref.shape[0]
-    half = here_latent.shape[0]
+    half = latent_ref.shape[0]
     queries = rows // heads
+    rep = rep_ref[0]
 
     for start in range(0, rows, block):
         rows_here = pl.ds(start, block)
 
         def causal(first, score):
-            block_rows = 2 * half
             j = first + lax.broadcasted_iota(jnp.int32, score.shape, 1)
             q = (start + lax.broadcasted_iota(jnp.int32, score.shape, 0)) // heads
-            return jnp.where(j <= block_rows - queries + q, score, masked_score)
-
-        rep = rep_ref[0]
+            return jnp.where(j <= 2 * half - queries + q, score, masked_score)
+
         pieces = [
-            (here_latent[...], here_rope[...], functools.partial(causal, rep * half), None),
+            (latent_ref[...], rope_ref[...], functools.partial(causal, rep * half), None),
             (there_latent[...], there_rope[...], functools.partial(causal, (1 - rep) * half), None),
         ]
         state = attend_rows(rows_here, query_ref, qrope_ref, pieces, scale, None)
@@ -150,42 +163,50 @@
 def attend_own(rep, query, query_rope, here, there, heads, scale):
     rows, width = query.shape
     out_shape = (
+        jax.ShapeDtypeStruct(query.shape, query.dtype),
         jax.ShapeDtypeStruct((rows, 1), jnp.float32),
         jax.ShapeDtypeStruct((rows, 1), jnp.float32),
         jax.ShapeDtypeStruct((rows, width), jnp.float32),
     )
-    return pl.pallas_call(
+    query, *state = pl.pallas_call(
         functools.partial(own_kernel, math.gcd(rows, 256), heads, scale),
         out_shape=out_shape,
-        in_specs=[in_smem] + [in_vmem] * 6,
-        out_specs=[in_vmem] * 3,
-        compiler_params=params(32),
+        in_specs=[in_smem, in_hbm, in_vmem, in_hbm, in_hbm, in_vmem, in_vmem],
+        out_specs=[in_vmem] * 4,
+        scratch_shapes=[
+            pltpu.VMEM(here[0].shape, here[0].dtype),
+            pltpu.VMEM(here[1].shape, here[1].dtype),
+            pltpu.SemaphoreType.DMA((3,)),
+        ],
+        compiler_params=params(10),
         cost_estimate=attention_cost(rows, 2 * here[0].shape[0], width),
         name="attend_own",
-    )(rep, query, query_rope, *here, *there)
-
-
-def biased_pieces(levels_of, bias_ref, refs, rope_width):
+    )(rep, kept_in_hbm(query), query_rope, *[kept_in_hbm(x) for x in here], *there)
+    return query, state
+
+
+def biased_pieces(levels_of, shard_ref, refs, rope_width):
     pieces = []
     for level, ref in zip(levels_of, refs):
         keys, ropes = read_piece(ref, rope_width)
-        pieces.append((keys, ropes, None, bias_ref[level]))
+        bias = jnp.where(shard_ref[0] >= 2**level, 0.0, masked_score)
+        pieces.append((keys, ropes, None, bias))
     return pieces
 
 
-def middle_kernel(block, levels_of, scale, bias_ref, query_ref, qrope_ref, *refs):
+def middle_kernel(block, levels_of, scale, shard_ref, query_ref, qrope_ref, *refs):
     count = len(levels_of)
     max_in, sum_in, out_in, max_ref, sum_ref, out_ref = refs[count:]
     rope_width = qrope_ref.shape[1]
     for start in range(0, query_ref.shape[0], block):
         rows_here = pl.ds(start, block)
-        pieces = biased_pieces(levels_of, bias_ref, refs[:count], rope_width)
+        pieces = biased_pieces(levels_of, shard_ref, refs[:count], rope_width)
         state = (max_in[rows_here, :], sum_in[rows_here, :], out_in[rows_here, :])
         state = attend_rows(rows_here, query_ref, qrope_ref, pieces, scale, state)
         max_ref[rows_here, :], sum_ref[rows_here, :], out_ref[rows_here, :] = state
 
 
-def attend_middle(bias, query, query_rope, pieces, levels_of, state, scale):
+def attend_middle(shard, query, query_rope, pieces, levels_of, state, scale):
     rows, width = query.shape
     keys = sum(piece.shape[0] for piece in pieces)
     return pl.pallas_call(
@@ -193,13 +214,15 @@
         out_shape=tuple(jax.ShapeDtypeStruct(s.shape, s.dtype) for s in state),
         in_specs=[in_smem] + [in_vmem] * (2 + len(pieces) + 3),
         out_specs=[in_vmem] * 3,
-        compiler_params=params(32),
+        compiler_params=params(10),
         cost_estimate=attention_cost(rows, keys, width),
         name="attend_middle",
-    )(bias, query, query_rope, *pieces, *state)
-
-
-def last_kernel(block, levels_of, heads, scale, peers, order_ref, bias_ref, query_ref, qrope_ref, *refs):
+    )(shard, query, query_rope, *pieces, *state)
+
+
+def last_kernel(
+    block, levels_of, heads, scale, columns, column_ref, rep_ref, shard_ref, query_ref, qrope_ref, *refs
+):
     count = len(levels_of)
     max_in, sum_in, out_in, up_ref, proj_ref, result_ref, norm_ref, exp_ref = refs[count:]
     rope_width = qrope_ref.shape[1]
@@ -208,7 +231,7 @@
     value = up_ref.shape[2]
     for start in range(0, rows, block):
         rows_here = pl.ds(start, block)
-        pieces = biased_pieces(levels_of, bias_ref, refs[:count], rope_width)
+        pieces = biased_pieces(levels_of, shard_ref, refs[:count], rope_width)
         state = (max_in[rows_here, :], sum_in[rows_here, :], out_in[rows_here, :])
         _, total, out = attend_rows(rows_here, query_ref, qrope_ref, pieces, scale, state)
         norm = out * (1.0 / total)
@@ -222,68 +245,73 @@
         attended = jnp.concatenate(tiles, axis=1)
         expanded = jnp.dot(attended, up_ref[head], preferred_element_type=jnp.float32)
         exp_ref[:, pl.ds(head * value, value)] = expanded.astype(jnp.bfloat16)
-    chunk = queries // peers
-    parts = [exp_ref[pl.ds(pl.multiple_of(order_ref[i] * chunk, chunk), chunk), :] for i in range(peers)]
+    chunk = queries // (2 * columns)
+    parts = []
+    for core in (1 - rep_ref[0], rep_ref[0]):
+        for by in range(1, columns + 1):
+            owner = lax.rem(column_ref[0] + by, columns) * 2 + core
+            parts.append(exp_ref[pl.ds(pl.multiple_of(owner * chunk, chunk), chunk), :])
     lhs = jnp.concatenate(parts, axis=0)
-    columns = proj_ref.shape[1]
-    step = math.gcd(columns, 512)
-    for column in range(0, columns, step):
-        piece = jnp.dot(lhs, proj_ref[:, pl.ds(column, step)], preferred_element_type=jnp.float32)
-        result_ref[:, pl.ds(column, step)] = piece.astype(result_ref.dtype)
-
-
-def attend_last(order, bias, query, query_rope, pieces, levels_of, state, scale, value_up, out_proj):
+    width_out = proj_ref.shape[1]
+    step = math.gcd(width_out, 512)
+    for start in range(0, width_out, step):
+        piece = jnp.dot(lhs, proj_ref[:, pl.ds(start, step)], preferred_element_type=jnp.float32)
+        result_ref[:, pl.ds(start, step)] = piece.astype(result_ref.dtype)
+
+
+def attend_last(columns, column, rep, shard, query, query_rope, pieces, levels_of, state, scale, value_up, out_proj):
     rows, width = query.shape
     heads = value_up.shape[0]
     queries = rows // heads
     keys = sum(piece.shape[0] for piece in pieces)
-    columns = out_proj.shape[1]
+    width_out = out_proj.shape[1]
     return pl.pallas_call(
         functools.partial(
-            last_kernel, math.gcd(rows, 256), tuple(levels_of), heads, scale, order.shape[0]
+            last_kernel, math.gcd(rows, 256), tuple(levels_of), heads, scale, columns
         ),
-        out_shape=jax.ShapeDtypeStruct((queries, columns), jnp.bfloat16),
-        in_specs=[in_smem, in_smem] + [in_vmem] * (2 + len(pieces) + 3 + 2),
+        out_shape=jax.ShapeDtypeStruct((queries, width_out), jnp.bfloat16),
+        in_specs=[in_smem] * 3 + [in_vmem] * (2 + len(pieces) + 3 + 2),
         out_specs=in_vmem,
         scratch_shapes=[
             pltpu.VMEM((width // lanes, rows, lanes), jnp.float32),
             pltpu.VMEM((queries, out_proj.shape[0]), jnp.bfloat16),
         ],
-        compiler_params=params(40),
+        compiler_params=params(12),
         cost_estimate=attention_cost(rows, keys, width),
         name="attend_last",
-    )(order, bias, query, query_rope, *pieces, *state, value_up, out_proj)
+    )(column, rep, shard, query, query_rope, *pieces, *state, value_up, out_proj)
 
 
 def shards(query_latent, query_rope, latent, key_rope, value_up, out_proj):
     queries, heads, width = query_latent.shape
     rope_width = key_rope.shape[0]
-    levels = min(4, lax.axis_size("seq") // 4 + 1)
+    levels = level_count(lax.axis_size("seq"))
     columns = lax.axis_size("head")
-    column = lax.axis_index("head")
-    rep = lax.axis_index("rep")
-    shard_index = lax.axis_index("seq")
+    column = lax.axis_index("head")[None]
+    rep = lax.axis_index("rep")[None]
+    shard = lax.axis_index("seq")[None]
+    column, rep, shard = lax.optimization_barrier((column, rep, shard))
     scale = (width + rope_width) ** (-0.5) * log2e
-    bias = jnp.stack(
-        [jnp.where(shard_index >= 2**level, 0.0, masked_score) for level in range(levels)]
-    ).astype(jnp.float32)
     query = query_latent.reshape(queries * heads, width)
     qrope = query_rope.reshape(queries * heads, rope_width)
 
-    part = pack_part(column[None], columns, latent, key_rope)
+    part = pack_part(column, columns, latent, key_rope)
     by_level = []
     moved = part
     for level in range(levels):
-        moved = shifted(moved, "seq", 1 if level == 0 else 2 ** (level - 1))
+        by = 1 if level == 0 else 2 ** (level - 1)
+        moved = shifted(moved, "seq", by, 0 if level == 0 else by)
         by_level.append(moved)
     there = (rotated(latent, "rep", 1), rotated(key_rope, "rep", 1))
-    state = attend_own(rep[None], query, qrope, (latent, key_rope), there, heads, scale)
+    query, state = attend_own(rep, query, qrope, (latent, key_rope), there, heads, scale)
 
     middle, middle_levels, last, last_levels = [], [], [], []
     for level in range(levels):
         direct = by_level[level]
-        crossed = [rotated(direct, "head", by) for by in range(1, columns)]
-        for index, piece in enumerate([direct] + crossed):
+        pieces = [direct]
+        for by in range(1, columns):
+            pieces.append(rotated(direct, "head", by))
+        for index, piece in enumerate(pieces):
             both = [piece, rotated(piece, "rep", 1)]
             if level == levels - 1 and index > 0:
                 last += both
@@ -291,12 +319,10 @@
             else:
                 middle += both
                 middle_levels += [level] * 2
-    state = attend_middle(bias, query, qrope, middle, middle_levels, state, scale)
-
-    chips = [(column + by) % columns for by in range(1, columns + 1)]
-    order = jnp.stack([chip * 2 + 1 - rep for chip in chips] + [chip * 2 + rep for chip in chips])
+    state = attend_middle(shard, query, qrope, middle, middle_levels, state, scale)
+
     partial = attend_last(
-        order, bias, query, qrope, last, last_levels, state, scale, value_up, out_proj
+        columns, column, rep, shard, query, qrope, last, last_levels, state, scale, value_up, out_proj
     )
     half = queries // 2
     arrived = rotated(partial[:half], "rep", 1)
@@ -308,10 +334,13 @@
         sums.append(kept[rows].astype(jnp.float32) + arrived[rows].astype(jnp.float32))
     result = sums[-1]
     for index in range(columns - 1):
-        result = result + rotated(sums[index].astype(jnp.bfloat16), "head", index + 1).astype(
-            jnp.float32
-        )
+        sent = sums[index].astype(jnp.bfloat16)
+        result = result + rotated(sent, "head", index + 1).astype(jnp.float32)
     return result.astype(jnp.bfloat16)
+
+
+def level_count(shards_along):
+    return min(4, shards_along // 4 + 1)
 
 
 def solution(mesh):
@@ -323,6 +352,7 @@
         P(("head", "rep"), None, None),
         P(("head", "rep"), None),
     )
+
     return jax.shard_map(
         shards,
         mesh=mesh,

time: 54.1 us -> 52.5 us (0.970)
  the two profiles are of different devices: /device:TPU:0 before, /device:TPU:10 now
where the time goes in v2:
time: 52.5 us; the launch traced here: 52.4 us
  waiting for transfers between devices  23.6 us (45%)
  Pallas kernels  16.6 us (32%)
  starting transfers between devices  9.96 us (19%)
  local copies, waits for them, and re-layouts  1.15 us (2%)
  other arithmetic  0.86 us (2%)
    ppermute x10, waiting for transfers between devices, rotated(): lax.ppermute(value, axis, [(i, (i + by) % peers) for i in range(peers)])  12.3 us
    ppermute x2, waiting for transfers between devices, shifted(): lax.ppermute(value, axis, [(i, i + by) for i in range(first, peers - by)])  11.3 us
    ppermute x2, starting transfers between devices, shifted(): lax.ppermute(value, axis, [(i, i + by) for i in range(first, peers - by)])  6.97 us
    pallas_call x1, Pallas kernels, attend_middle(): pl.pallas_call(functools.partial(middle_kernel, math.gcd(rows, 256), tupl...  5.93 us
    pallas_call x1, Pallas kernels, attend_own(): pl.pallas_call(functools.partial(own_kernel, math.gcd(rows, 256), heads,...  5.13 us
    pallas_call x1, Pallas kernels, attend_last(): pl.pallas_call(functools.partial(last_kernel, math.gcd(rows, 256), tuple(...  4.58 us
    ppermute x10, starting transfers between devices, rotated(): lax.ppermute(value, axis, [(i, (i + by) % peers) for i in range(peers)])  2.99 us
    reshape x1, local copies, waits for them, and re-layouts, shards(): qrope = query_rope.reshape(queries * heads, rope_width)  1.1 us
  transfers between devices with their start and end apart: 12, of which 5 were waited for; matrix products, arithmetic and copies ran while one was open for 2% of the time, Pallas kernels for 21%

profile of v2, /device:TPU:10, one launch (start us, length us, event | category | flops | bytes accessed | tf_op | source)
XLA Modules:
  0.0 52.4 jit_solution(978882299453289420)
XLA Ops:
  0.0 1.0 %pack_part.1 = bf16[288,512]{1,0:T(8,128)(2,1)S(1)} custom-call(s32[1]{0:T(128)} %bitcast.part_ref.column_ref, bf16[512,512]{1,0:T(8,128)(2,1)} %latent_ref.1, bf16[64,512]{1,0:T(8,128)(2,1)} %rope_ref.1), custom_call_target="tpu_custom_call" | custom-call | bytes 600000 | tf_op jit(solution)/shard_map/pack_part/pallas_call | solution.py:70
  1.0 3.5 %collective-permute-start.2 = (bf16[288,512]{1,0:T(8,128)(2,1)S(1)}, bf16[288,512]{1,0:T(8,128)(2,1)S(1)}, u32[]{:S(2)}, u32[]{:S(2)}) collective-permute-start(bf16[288,512]{1,0:T(8,128)(2,1)S(1)} %pack_part.1), channel_id=1, source_target_pairs={{0,4},{4,8},{8,12},{1,5},{5,9},{9,13},{2,6},{6,10},{10,14},{3,7},{... | collective-permute-start | bytes 884744 | tf_op jit(solution)/shard_map/ppermute | solution.py:31
  4.5 0.1 collective-permute-start
  4.6 7.1 %collective-permute-done.2.refs_0_ = bf16[288,512]{1,0:T(8,128)(2,1)S(1)} collective-permute-done((bf16[288,512]{1,0:T(8,128)(2,1)S(1)}, bf16[288,512]{1,0:T(8,128)(2,1)S(1)}, u32[]{:S(2)}, u32[]{:S(2)}) %collective-permute-start.2) | collective-permute-done | bytes 294944 | tf_op jit(solution)/shard_map/ppermute | solution.py:31
  11.6 3.5 %collective-permute-start.3 = (bf16[288,512]{1,0:T(8,128)(2,1)S(1)}, bf16[288,512]{1,0:T(8,128)(2,1)S(1)}, u32[]{:S(2)}, u32[]{:S(2)}) collective-permute-start(bf16[288,512]{1,0:T(8,128)(2,1)S(1)} %collective-permute-done.2.refs_0_), channel_id=1, source_target_pairs={{4,8},{8,12},{5,9},{9,13},{6,10},{10,14},{7,11},{11,15},{20,24},{2... | collective-permute-start | bytes 884744 | tf_op jit(solution)/shard_map/ppermute | solution.py:31
  15.1 0.6 %collective-permute-start.7 = (bf16[288,512]{1,0:T(8,128)(2,1)S(1)}, bf16[288,512]{1,0:T(8,128)(2,1)S(1)}, u32[]{:S(2)}, u32[]{:S(2)}) collective-permute-start(bf16[288,512]{1,0:T(8,128)(2,1)S(1)} %collective-permute-done.2.refs_0_), channel_id=1, source_target_pairs={{0,2},{2,0},{1,3},{3,1},{4,6},{6,4},{5,7},{7,5},{8,10},{10,8},{9,1... | collective-permute-start | bytes 884744 | tf_op jit(solution)/shard_map/ppermute | solution.py:36
  15.7 0.0 collective-permute-start.1
  15.7 0.5 collective-permute-start.6
  16.2 4.3 %collective-permute-done.3.refs_4_ = bf16[288,512]{1,0:T(8,128)(2,1)S(1)} collective-permute-done((bf16[288,512]{1,0:T(8,128)(2,1)S(1)}, bf16[288,512]{1,0:T(8,128)(2,1)S(1)}, u32[]{:S(2)}, u32[]{:S(2)}) %collective-permute-start.3) | collective-permute-done | bytes 294944 | tf_op jit(solution)/shard_map/ppermute | solution.py:31
  20.5 0.5 %collective-permute-start.4 = (bf16[288,512]{1,0:T(8,128)(2,1)S(1)}, bf16[288,512]{1,0:T(8,128)(2,1)S(1)}, u32[]{:S(2)}, u32[]{:S(2)}) collective-permute-start(bf16[288,512]{1,0:T(8,128)(2,1)S(1)} %collective-permute-done.3.refs_4_), channel_id=1, source_target_pairs={{0,2},{2,0},{1,3},{3,1},{4,6},{6,4},{5,7},{7,5},{8,10},{10,8},{9,1... | collective-permute-start | bytes 884744 | tf_op jit(solution)/shard_map/ppermute | solution.py:36
  21.0 0.0 collective-permute-done.1.refs_1_
  21.0 0.0 collective-permute-start.9
  21.0 3.3 %collective-permute-done.7.refs_2_ = bf16[288,512]{1,0:T(8,128)(2,1)S(1)} collective-permute-done((bf16[288,512]{1,0:T(8,128)(2,1)S(1)}, bf16[288,512]{1,0:T(8,128)(2,1)S(1)}, u32[]{:S(2)}, u32[]{:S(2)}) %collective-permute-start.7) | collective-permute-done | bytes 294944 | tf_op jit(solution)/shard_map/ppermute | solution.py:36
  24.4 0.0 collective-permute-start.8
  24.4 1.1 %reshape.7.qrope_ref = bf16[1024,64]{1,0:T(8,128)(2,1)S(1)} reshape(bf16[128,512]{1,0:T(8,128)(2,1)} %param.7) | data formatting | bytes 262144 | tf_op jit(solution)/shard_map/reshape | solution.py:296
  25.5 0.0 collective-permute-done.refs_0_
  25.5 5.1 %attend_own.1 = (bf16[1024,512]{1,0:T(8,128)(2,1)S(1)}, f32[1024,1]{1,0:T(8,128)S(1)}, f32[1024,1]{1,0:T(8,128)S(1)}, f32[1024,512]{1,0:T(8,128)S(1)}) custom-call(s32[1]{0:T(128)} %bitcast.1.rep_ref, bf16[1024,512]{1,0:T(8,128)(2,1)} %bitcast.6, bf16[1024,64]{1,0:T(8,128)(2,1)S(1)} %reshape.7.qrope_ref, bf16[512,512]{1,0:T(8,128)(2,1)} %latent_ref.1, ...), custom_call_target="tpu_custom_call" | custom-call | flops 2147483648 | bytes 1048576 | tf_op jit(solution)/shard_map/attend_own/pallas_call | solution.py:171
  30.6 0.0 collective-permute-done.4.refs_0_
  30.7 0.6 %collective-permute-start.5 = (bf16[288,512]{1,0:T(8,128)(2,1)S(1)}, bf16[288,512]{1,0:T(8,128)(2,1)S(1)}, u32[]{:S(2)}, u32[]{:S(2)}) collective-permute-start(bf16[288,512]{1,0:T(8,128)(2,1)S(1)} %collective-permute-done.4.refs_0_), channel_id=1, source_target_pairs={{0,1},{1,0},{2,3},{3,2},{4,5},{5,4},{6,7},{7,6},{8,9},{9,8},{10,11... | collective-permute-start | bytes 884744 | tf_op jit(solution)/shard_map/ppermute | solution.py:36
  31.2 0.0 collective-permute-done.6.refs_1_
  31.2 0.0 collective-permute-done.9.refs_5_
  31.2 0.0 collective-permute-done.8.refs_3_
  31.2 0.0 slice-start
  31.3 0.0 slice-start.1
  31.3 0.0 copy-start
  31.3 5.9 %attend_middle.1 = (f32[1024,1]{1,0:T(8,128)S(1)}, f32[1024,1]{1,0:T(8,128)S(1)}, f32[1024,512]{1,0:T(8,128)S(1)}) custom-call(s32[1]{0:T(128)} %bitcast.2.shard_ref, bf16[1024,512]{1,0:T(8,128)(2,1)S(1)} %get-tuple-element.18.query_ref, bf16[1024,64]{1,0:T(8,128)(2,1)S(1)} %reshape.7.qrope_ref, bf16[288,512]{1,0:T(8,128)(2,1)S(1)} %collective-permute-done.2.refs_0_, ...), custom_call_target="tpu_custom_call" | custom-call | flops 3623878656 | bytes 1048576 | tf_op jit(solution)/shard_map/attend_middle/pallas_call | solution.py:212
  37.2 0.0 collective-permute-done.5.refs_1_
  37.2 0.0 slice-done
  37.2 0.0 slice-done.1
  37.3 0.0 copy-done
  37.3 4.6 %attend_last.1 = bf16[128,3584]{1,0:T(8,128)(2,1)S(1)} custom-call(s32[1]{0:T(128)} %bitcast.part_ref.column_ref, s32[1]{0:T(128)} %bitcast.1.rep_ref, s32[1]{0:T(128)} %bitcast.2.shard_ref, bf16[1024,512]{1,0:T(8,128)(2,1)S(1)} %get-tuple-element.18.query_ref, bf16[1024,64]{1,0:T(8,128)(2,1)S(1)} %reshape.7.qrope_ref, ...), custom_call_target="tpu_custom_call" | custom-call | flops 1207959552 | bytes 1048576 | tf_op jit(solution)/shard_map/attend_last/pallas_call | solution.py:268
  41.9 0.1 collective-permute-start.10
  42.0 1.8 %collective-permute-done.10 = bf16[64,3584]{1,0:T(8,128)(2,1)S(1)} collective-permute-done((bf16[64,3584]{1,0:T(8,128)(2,1)S(1)}, bf16[64,3584]{1,0:T(8,128)(2,1)S(1)}, u32[]{:S(2)}, u32[]{:S(2)}) %collective-permute-start.10) | collective-permute-done | bytes 458784 | tf_op jit(solution)/shard_map/ppermute | solution.py:36
  43.8 0.1 add_convert_fusion.1
  43.8 0.6 %collective-permute-start.11 = (bf16[32,3584]{1,0:T(8,128)(2,1)S(1)}, bf16[32,3584]{1,0:T(8,128)(2,1)S(1)}, u32[]{:S(2)}, u32[]{:S(2)}) collective-permute-start(bf16[32,3584]{1,0:T(8,128)(2,1)S(1)} %add_convert_fusion.1), channel_id=1, source_target_pairs={{0,2},{2,0},{1,3},{3,1},{4,6},{6,4},{5,7},{7,5},{8,10},{10,8},{9,1... | collective-permute-start | bytes 688136 | tf_op jit(solution)/shard_map/ppermute | solution.py:36
  44.4 7.1 %collective-permute-done.11 = bf16[32,3584]{1,0:T(8,128)(2,1)S(1)} collective-permute-done((bf16[32,3584]{1,0:T(8,128)(2,1)S(1)}, bf16[32,3584]{1,0:T(8,128)(2,1)S(1)}, u32[]{:S(2)}, u32[]{:S(2)}) %collective-permute-start.11) | collective-permute-done | bytes 229408 | tf_op jit(solution)/shard_map/ppermute | solution.py:36
  51.6 0.8 %add_convert_fusion = bf16[32,3584]{1,0:T(8,128)(2,1)} fusion(bf16[32,3584]{1,0:T(8,128)(2,1)S(1)} %collective-permute-done.11, bf16[64,3584]{1,0:T(8,128)(2,1)S(1)} %collective-permute-done.10, bf16[128,3584]{1,0:T(8,128)(2,1)S(1)} %attend_last.1), kind=kLoop, calls=%fused_computation | loop fusion | flops 688128 | bytes 917504 | tf_op jit(solution)/shard_map/convert_element_type | solution.py:339
  (2 shorter events, 0.0 us)
Async XLA Ops:
  1.0 10.6 %collective-permute-start.2 = (bf16[288,512]{1,0:T(8,128)(2,1)S(1)}, bf16[288,512]{1,0:T(8,128)(2,1)S(1)}, u32[]{:S(2)}, u32[]{:S(2)}) collective-permute-start(bf16[288,512]{1,0:T(8,128)(2,1)S(1)} %pack_part.1), channel_id=1, source_target_pairs={{0,4},{4,8},{8,12},{1,5},{5,9},{9,13},{2,6},{6,10},{10,14},{3,7},{... | collective-permute-start | bytes 884744 | tf_op jit(solution)/shard_map/ppermute | solution.py:31
  4.5 21.0 %collective-permute-start = (bf16[512,512]{1,0:T(8,128)(2,1)}, bf16[512,512]{1,0:T(8,128)(2,1)S(1)}, u32[]{:S(2)}, u32[]{:S(2)}) collective-permute-start(bf16[512,512]{1,0:T(8,128)(2,1)} %latent_ref.1), channel_id=1, source_target_pairs={{0,1},{1,0},{2,3},{3,2},{4,5},{5,4},{6,7},{7,6},{8,9},{9,8},{10,11... | collective-permute-start | bytes 1572872 | tf_op jit(solution)/shard_map/ppermute | solution.py:36
  11.6 8.9 %collective-permute-start.3 = (bf16[288,512]{1,0:T(8,128)(2,1)S(1)}, bf16[288,512]{1,0:T(8,128)(2,1)S(1)}, u32[]{:S(2)}, u32[]{:S(2)}) collective-permute-start(bf16[288,512]{1,0:T(8,128)(2,1)S(1)} %collective-permute-done.2.refs_0_), channel_id=1, source_target_pairs={{4,8},{8,12},{5,9},{9,13},{6,10},{10,14},{7,11},{11,15},{20,24},{2... | collective-permute-start | bytes 884744 | tf_op jit(solution)/shard_map/ppermute | solution.py:31
  15.1 9.3 %collective-permute-start.7 = (bf16[288,512]{1,0:T(8,128)(2,1)S(1)}, bf16[288,512]{1,0:T(8,128)(2,1)S(1)}, u32[]{:S(2)}, u32[]{:S(2)}) collective-permute-start(bf16[288,512]{1,0:T(8,128)(2,1)S(1)} %collective-permute-done.2.refs_0_), channel_id=1, source_target_pairs={{0,2},{2,0},{1,3},{3,1},{4,6},{6,4},{5,7},{7,5},{8,10},{10,8},{9,1... | collective-permute-start | bytes 884744 | tf_op jit(solution)/shard_map/ppermute | solution.py:36
  15.7 5.3 %collective-permute-start.1 = (bf16[64,512]{1,0:T(8,128)(2,1)}, bf16[64,512]{1,0:T(8,128)(2,1)S(1)}, u32[]{:S(2)}, u32[]{:S(2)}) collective-permute-start(bf16[64,512]{1,0:T(8,128)(2,1)} %rope_ref.1), channel_id=1, source_target_pairs={{0,1},{1,0},{2,3},{3,2},{4,5},{5,4},{6,7},{7,6},{8,9},{9,8},{10,11... | collective-permute-start | bytes 196616 | tf_op jit(solution)/shard_map/ppermute | solution.py:36
  15.7 15.5 %collective-permute-start.6 = (bf16[288,512]{1,0:T(8,128)(2,1)S(1)}, bf16[288,512]{1,0:T(8,128)(2,1)S(1)}, u32[]{:S(2)}, u32[]{:S(2)}) collective-permute-start(bf16[288,512]{1,0:T(8,128)(2,1)S(1)} %collective-permute-done.2.refs_0_), channel_id=1, source_target_pairs={{0,1},{1,0},{2,3},{3,2},{4,5},{5,4},{6,7},{7,6},{8,9},{9,8},{10,11... | collective-permute-start | bytes 884744 | tf_op jit(solution)/shard_map/ppermute | solution.py:36
  20.5 10.1 %collective-permute-start.4 = (bf16[288,512]{1,0:T(8,128)(2,1)S(1)}, bf16[288,512]{1,0:T(8,128)(2,1)S(1)}, u32[]{:S(2)}, u32[]{:S(2)}) collective-permute-start(bf16[288,512]{1,0:T(8,128)(2,1)S(1)} %collective-permute-done.3.refs_4_), channel_id=1, source_target_pairs={{0,2},{2,0},{1,3},{3,1},{4,6},{6,4},{5,7},{7,5},{8,10},{10,8},{9,1... | collective-permute-start | bytes 884744 | tf_op jit(solution)/shard_map/ppermute | solution.py:36
  21.0 10.2 %collective-permute-start.9 = (bf16[288,512]{1,0:T(8,128)(2,1)S(1)}, bf16[288,512]{1,0:T(8,128)(2,1)S(1)}, u32[]{:S(2)}, u32[]{:S(2)}) collective-permute-start(bf16[288,512]{1,0:T(8,128)(2,1)S(1)} %collective-permute-done.3.refs_4_), channel_id=1, source_target_pairs={{0,1},{1,0},{2,3},{3,2},{4,5},{5,4},{6,7},{7,6},{8,9},{9,8},{10,11... | collective-permute-start | bytes 884744 | tf_op jit(solution)/shard_map/ppermute | solution.py:36
  24.4 6.9 %collective-permute-start.8 = (bf16[288,512]{1,0:T(8,128)(2,1)S(1)}, bf16[288,512]{1,0:T(8,128)(2,1)S(1)}, u32[]{:S(2)}, u32[]{:S(2)}) collective-permute-start(bf16[288,512]{1,0:T(8,128)(2,1)S(1)} %collective-permute-done.7.refs_2_), channel_id=1, source_target_pairs={{0,1},{1,0},{2,3},{3,2},{4,5},{5,4},{6,7},{7,6},{8,9},{9,8},{10,11... | collective-permute-start | bytes 884744 | tf_op jit(solution)/shard_map/ppermute | solution.py:36
  30.7 6.6 %collective-permute-start.5 = (bf16[288,512]{1,0:T(8,128)(2,1)S(1)}, bf16[288,512]{1,0:T(8,128)(2,1)S(1)}, u32[]{:S(2)}, u32[]{:S(2)}) collective-permute-start(bf16[288,512]{1,0:T(8,128)(2,1)S(1)} %collective-permute-done.4.refs_0_), channel_id=1, source_target_pairs={{0,1},{1,0},{2,3},{3,2},{4,5},{5,4},{6,7},{7,6},{8,9},{9,8},{10,11... | collective-permute-start | bytes 884744 | tf_op jit(solution)/shard_map/ppermute | solution.py:36
  31.2 6.0 %slice-start = ((s8[7340032]{0:T(1024)(128)(4,1)}), s8[4194304]{0:T(1024)(128)(4,1)S(1)}, s32[]{:S(2)}) async-start(s8[7340032]{0:T(1024)(128)(4,1)} %bitcast.4), calls=%async_computation | async-start | bytes 8388608
  31.3 6.0 %slice-start.1 = ((s8[7340032]{0:T(1024)(128)(4,1)}), s8[3145728]{0:T(1024)(128)(4,1)S(1)}, s32[]{:S(2)}) async-start(s8[7340032]{0:T(1024)(128)(4,1)} %bitcast.4), calls=%async_computation.1 | async-start | bytes 6291456
  31.3 6.0 %copy-start = (bf16[8,512,128]{2,1,0:T(8,128)(2,1)S(1)}, bf16[8,512,128]{2,1,0:T(8,128)(2,1)}, u32[]{:S(2)}) copy-start(bf16[8,512,128]{2,1,0:T(8,128)(2,1)} %refs_5_.1) | copy-start | bytes 3145732
  41.9 1.9 %collective-permute-start.10 = (bf16[64,3584]{1,0:T(8,128)(2,1)S(1)}, bf16[64,3584]{1,0:T(8,128)(2,1)S(1)}, u32[]{:S(2)}, u32[]{:S(2)}) collective-permute-start(bf16[64,3584]{1,0:T(8,128)(2,1)S(1)} %slice.24), channel_id=1, source_target_pairs={{0,1},{1,0},{2,3},{3,2},{4,5},{5,4},{6,7},{7,6},{8,9},{9,8},{10,11... | collective-permute-start | bytes 1376264 | tf_op jit(solution)/shard_map/ppermute | solution.py:36
  43.8 7.7 %collective-permute-start.11 = (bf16[32,3584]{1,0:T(8,128)(2,1)S(1)}, bf16[32,3584]{1,0:T(8,128)(2,1)S(1)}, u32[]{:S(2)}, u32[]{:S(2)}) collective-permute-start(bf16[32,3584]{1,0:T(8,128)(2,1)S(1)} %add_convert_fusion.1), channel_id=1, source_target_pairs={{0,2},{2,0},{1,3},{3,1},{4,6},{6,4},{5,7},{7,5},{8,10},{10,8},{9,1... | collective-permute-start | bytes 688136 | tf_op jit(solution)/shard_map/ppermute | solution.py:36

commit v3 on v2

--- a/solution.py
+++ b/solution.py
@@ -36,57 +36,60 @@
     return lax.ppermute(value, axis, [(i, (i + by) % peers) for i in range(peers)])
 
 
-def pack_kernel(part_ref, latent_ref, rope_ref, packed_ref, sems):
+def split_rows(packed_rows, width, rope_width):
+    rows = packed_rows * width // (width + rope_width)
+    folds = width // rows
+    return rows, folds, rope_width // folds
+
+
+def pack_kernel(part_ref, latent_ref, rope_ref, *refs):
+    packed_refs, sems = refs[:-1], refs[-1]
     width = latent_ref.shape[1]
-    rope_width = rope_ref.shape[0]
-    rows = packed_ref.shape[0] * width // (width + rope_width)
-    folds = width // rows
-    group = rope_width // folds
-    start = pl.multiple_of(part_ref[0] * rows, rows)
-    copies = [
-        pltpu.make_async_copy(
-            latent_ref.at[pl.ds(start, rows), :], packed_ref.at[pl.ds(0, rows), :], sems.at[0]
-        )
-    ]
-    for fold in range(folds):
-        copies.append(
-            pltpu.make_async_copy(
-                rope_ref.at[pl.ds(fold * group, group), pl.ds(start, rows)],
-                packed_ref.at[pl.ds(rows, group), pl.ds(fold * rows, rows)],
-                sems.at[fold + 1],
+    rows, folds, group = split_rows(packed_refs[0].shape[0], width, rope_ref.shape[0])
+    copies = []
+    for chunk, packed_ref in enumerate(packed_refs):
+        start = pl.multiple_of((part_ref[0] * len(packed_refs) + chunk) * rows, rows)
+        moves = [(latent_ref.at[pl.ds(start, rows), :], packed_ref.at[pl.ds(0, rows), :])]
+        for fold in range(folds):
+            moves.append(
+                (
+                    rope_ref.at[pl.ds(fold * group, group), pl.ds(start, rows)],
+                    packed_ref.at[pl.ds(rows, group), pl.ds(fold * rows, rows)],
+                )
             )
-        )
+        for move in moves:
+            copies.append(pltpu.make_async_copy(*move, sems.at[len(copies)]))
     for copy in copies:
         copy.start()
     for copy in copies:
         copy.wait()
 
 
-def pack_part(part, parts, latent, key_rope):
-    rows = latent.shape[0] // parts
+def pack_part(part, parts, chunks, latent, key_rope):
     width = latent.shape[1]
+    rows = latent.shape[0] // parts // chunks
     folds = width // rows
-    group = key_rope.shape[0] // folds
+    packed = jax.ShapeDtypeStruct((rows + key_rope.shape[0] // folds, width), latent.dtype)
     return pl.pallas_call(
         pack_kernel,
-        out_shape=jax.ShapeDtypeStruct((rows + group, width), latent.dtype),
+        out_shape=[packed] * chunks,
         in_specs=[in_smem, in_hbm, in_hbm],
-        out_specs=in_vmem,
-        scratch_shapes=[pltpu.SemaphoreType.DMA((folds + 1,))],
+        out_specs=[in_vmem] * chunks,
+        scratch_shapes=[pltpu.SemaphoreType.DMA((chunks * (folds + 1),))],
         compiler_params=params(4),
         cost_estimate=pl.CostEstimate(flops=0, bytes_accessed=600000, transcendentals=0),
         name="pack_part",
     )(part, kept_in_hbm(latent), kept_in_hbm(key_rope))
 
 
-def read_piece(ref, rope_width):
-    width = ref.shape[1]
-    rows = ref.shape[0] * width // (width + rope_width)
-    folds = width // rows
-    group = rope_width // folds
-    keys = ref[pl.ds(0, rows), :]
-    ropes = [ref[pl.ds(rows, group), pl.ds(fold * rows, rows)] for fold in range(folds)]
-    return keys, jnp.concatenate(ropes, axis=0)
+def joined(refs, rope_width):
+    keys, ropes = [], []
+    for ref in refs:
+        rows, folds, group = split_rows(ref.shape[0], ref.shape[1], rope_width)
+        keys.append(ref[pl.ds(0, rows), :])
+        parts = [ref[pl.ds(rows, group), pl.ds(fold * rows, rows)] for fold in range(folds)]
+        ropes.append(jnp.concatenate(parts, axis=0))
+    return jnp.concatenate(keys, axis=0), jnp.concatenate(ropes, axis=1)
 
 
 def attend_rows(rows_here, query_ref, rope_ref, pieces, scale, state):
@@ -185,53 +188,58 @@
     return query, state
 
 
-def biased_pieces(levels_of, shard_ref, refs, rope_width):
+def biased_pieces(counts, shard_ref, refs, rope_width):
     pieces = []
-    for level, ref in zip(levels_of, refs):
-        keys, ropes = read_piece(ref, rope_width)
+    first = 0
+    for level, count in counts:
+        keys, ropes = joined(refs[first : first + count], rope_width)
+        first += count
         bias = jnp.where(shard_ref[0] >= 2**level, 0.0, masked_score)
         pieces.append((keys, ropes, None, bias))
     return pieces
 
 
-def middle_kernel(block, levels_of, scale, shard_ref, query_ref, qrope_ref, *refs):
-    count = len(levels_of)
+def counted(refs_of):
+    counts = tuple((level, len(refs)) for level, refs in sorted(refs_of.items()))
+    return counts, [ref for _, refs in sorted(refs_of.items()) for ref in refs]
+
+
+def middle_kernel(block, counts, scale, shard_ref, query_ref, qrope_ref, *refs):
+    count = sum(count for _, count in counts)
     max_in, sum_in, out_in, max_ref, sum_ref, out_ref = refs[count:]
-    rope_width = qrope_ref.shape[1]
+    pieces = biased_pieces(counts, shard_ref, refs[:count], qrope_ref.shape[1])
     for start in range(0, query_ref.shape[0], block):
         rows_here = pl.ds(start, block)
-        pieces = biased_pieces(levels_of, shard_ref, refs[:count], rope_width)
         state = (max_in[rows_here, :], sum_in[rows_here, :], out_in[rows_here, :])
         state = attend_rows(rows_here, query_ref, qrope_ref, pieces, scale, state)
         max_ref[rows_here, :], sum_ref[rows_here, :], out_ref[rows_here, :] = state
 
 
-def attend_middle(shard, query, query_rope, pieces, levels_of, state, scale):
+def attend_middle(shard, query, query_rope, refs_of, state, scale):
     rows, width = query.shape
-    keys = sum(piece.shape[0] for piece in pieces)
+    counts, refs = counted(refs_of)
+    keys = sum(ref.shape[0] for ref in refs)
     return pl.pallas_call(
-        functools.partial(middle_kernel, math.gcd(rows, 256), tuple(levels_of), scale),
+        functools.partial(middle_kernel, math.gcd(rows, 256), counts, scale),
         out_shape=tuple(jax.ShapeDtypeStruct(s.shape, s.dtype) for s in state),
-        in_specs=[in_smem] + [in_vmem] * (2 + len(pieces) + 3),
+        in_specs=[in_smem] + [in_vmem] * (2 + len(refs) + 3),
         out_specs=[in_vmem] * 3,
-        compiler_params=params(10),
+        compiler_params=params(12),
         cost_estimate=attention_cost(rows, keys, width),
-        name="attend_middle",
-    )(shard, query, query_rope, *pieces, *state)
+    )(shard, query, query_rope, *refs, *state)
 
 
 def last_kernel(
-    block, levels_of, heads, scale, columns, column_ref, rep_ref, shard_ref, query_ref, qrope_ref, *refs
+    block, counts, heads, scale, columns, column_ref, rep_ref, shard_ref, query_ref, qrope_ref, *refs
 ):
-    count = len(levels_of)
+    count = sum(count for _, count in counts)
     max_in, sum_in, out_in, up_ref, proj_ref, result_ref, norm_ref, exp_ref = refs[count:]
-    rope_width = qrope_ref.shape[1]
     rows, width = query_ref.shape
     queries = rows // heads
     value = up_ref.shape[2]
+    pieces = biased_pieces(counts, shard_ref, refs[:count], qrope_ref.shape[1])
     for start in range(0, rows, block):
         rows_here = pl.ds(start, block)
-        pieces = biased_pieces(levels_of, shard_ref, refs[:count], rope_width)
         state = (max_in[rows_here, :], sum_in[rows_here, :], out_in[rows_here, :])
         _, total, out = attend_rows(rows_here, query_ref, qrope_ref, pieces, scale, state)
         norm = out * (1.0 / total)
@@ -259,18 +267,21 @@
         result_ref[:, pl.ds(start, step)] = piece.astype(result_ref.dtype)
 
 
-def attend_last(columns, column, rep, shard, query, query_rope, pieces, levels_of, state, scale, value_up, out_proj):
+def attend_last(
+    columns, column, rep, shard, query, query_rope, refs_of, state, scale, value_up, out_proj
+):
+    counts, refs = counted(refs_of)
     rows, width = query.shape
     heads = value_up.shape[0]
     queries = rows // heads
-    keys = sum(piece.shape[0] for piece in pieces)
+    keys = sum(ref.shape[0] for ref in refs)
     width_out = out_proj.shape[1]
     return pl.pallas_call(
         functools.partial(
-            last_kernel, math.gcd(rows, 256), tuple(levels_of), heads, scale, columns
+            last_kernel, math.gcd(rows, 256), counts, heads, scale, columns
         ),
         out_shape=jax.ShapeDtypeStruct((queries, width_out), jnp.bfloat16),
-        in_specs=[in_smem] * 3 + [in_vmem] * (2 + len(pieces) + 3 + 2),
+        in_specs=[in_smem] * 3 + [in_vmem] * (2 + len(refs) + 3 + 2),
         out_specs=in_vmem,
         scratch_shapes=[
             pltpu.VMEM((width // lanes, rows, lanes), jnp.float32),
@@ -279,7 +290,7 @@
         compiler_params=params(12),
         cost_estimate=attention_cost(rows, keys, width),
         name="attend_last",
-    )(column, rep, shard, query, query_rope, *pieces, *state, value_up, out_proj)
+    )(column, rep, shard, query, query_rope, *refs, *state, value_up, out_proj)
 
 
 def shards(query_latent, query_rope, latent, key_rope, value_up, out_proj):
@@ -295,34 +306,31 @@
     query = query_latent.reshape(queries * heads, width)
     qrope = query_rope.reshape(queries * heads, rope_width)
 
-    part = pack_part(column, columns, latent, key_rope)
-    by_level = []
-    moved = part
+    chunks = chunk_count(latent.shape[0] // columns)
+    direct = pack_part(column, columns, chunks, latent, key_rope)
+    there = (rotated(latent, "rep", 1), rotated(key_rope, "rep", 1))
+    query, state = attend_own(rep, query, qrope, (latent, key_rope), there, heads, scale)
+
+    first, middle, last = {}, {}, {}
     for level in range(levels):
         by = 1 if level == 0 else 2 ** (level - 1)
-        moved = shifted(moved, "seq", by, 0 if level == 0 else by)
-        by_level.append(moved)
-    there = (rotated(latent, "rep", 1), rotated(key_rope, "rep", 1))
-    query, state = attend_own(rep, query, qrope, (latent, key_rope), there, heads, scale)
-
-    middle, middle_levels, last, last_levels = [], [], [], []
-    for level in range(levels):
-        direct = by_level[level]
-        pieces = [direct]
-        for by in range(1, columns):
-            pieces.append(rotated(direct, "head", by))
-        for index, piece in enumerate(pieces):
-            both = [piece, rotated(piece, "rep", 1)]
-            if level == levels - 1 and index > 0:
-                last += both
-                last_levels += [level] * 2
-            else:
-                middle += both
-                middle_levels += [level] * 2
-    state = attend_middle(shard, query, qrope, middle, middle_levels, state, scale)
-
+        direct = [shifted(piece, "seq", by, 0 if level == 0 else by) for piece in direct]
+        for chunk, piece in enumerate(direct):
+            for index in range(columns):
+                if index:
+                    moved = rotated(piece, "head", index)
+                else:
+                    moved = piece
+                both = [moved, rotated(moved, "rep", 1)]
+                crossed = index > 0
+                final = level == levels - 1 and crossed == (columns > 1)
+                stage = last if final else middle if level or crossed else first
+                stage.setdefault(level, []).extend(both)
+    for refs_of in (first, middle):
+        if refs_of:
+            state = attend_middle(shard, query, qrope, refs_of, state, scale)
     partial = attend_last(
-        columns, column, rep, shard, query, qrope, last, last_levels, state, scale, value_up, out_proj
+        columns, column, rep, shard, query, qrope, last, state, scale, value_up, out_proj
     )
     half = queries // 2
     arrived = rotated(partial[:half], "rep", 1)
@@ -343,6 +351,10 @@
     return min(4, shards_along // 4 + 1)
 
 
+def chunk_count(rows):
+    return 2 if rows % (2 * lanes) == 0 else 1
+
+
 def solution(mesh):
     placed = (
         P(("grp", "seq"), ("head", "rep"), None),

time: 52.5 us -> 61.2 us (1.17)
  the two profiles are of different devices: /device:TPU:10 before, /device:TPU:8 now
where the time goes in v3:
time: 61.2 us; the launch traced here: 60.9 us
  starting transfers between devices  21 us (34%)
  waiting for transfers between devices  19.8 us (32%)
  Pallas kernels  17.9 us (29%)
  local copies, waits for them, and re-layouts  1.16 us (2%)
  other arithmetic  0.83 us (1%)
    ppermute x16, waiting for transfers between devices, rotated(): lax.ppermute(value, axis, [(i, (i + by) % peers) for i in range(peers)])  15.1 us
    ppermute x4, starting transfers between devices, shifted(): lax.ppermute(value, axis, [(i, i + by) for i in range(first, peers - by)])  13.9 us
    ppermute x16, starting transfers between devices, rotated(): lax.ppermute(value, axis, [(i, (i + by) % peers) for i in range(peers)])  7.18 us
    pallas_call x2, Pallas kernels, attend_middle(): pl.pallas_call(functools.partial(middle_kernel, math.gcd(rows, 256), coun...  7.1 us
    pallas_call x1, Pallas kernels, attend_own(): pl.pallas_call(functools.partial(own_kernel, math.gcd(rows, 256), heads,...  5.14 us
    ppermute x4, waiting for transfers between devices, shifted(): lax.ppermute(value, axis, [(i, i + by) for i in range(first, peers - by)])  4.63 us
    pallas_call x1, Pallas kernels, attend_last(): pl.pallas_call(functools.partial(last_kernel, math.gcd(rows, 256), counts...  4.58 us
  transfers between devices with their start and end apart: 20, of which 8 were waited for; matrix products, arithmetic and copies ran while one was open for 2% of the time, Pallas kernels for 22%

profile of v3, /device:TPU:8, one launch (start us, length us, event | category | flops | bytes accessed | tf_op | source)
XLA Modules:
  0.0 60.9 jit_solution(15155979396430397064)
XLA Ops:
  0.0 0.0 collective-permute-start
  0.0 1.1 %pack_part.1 = (bf16[144,512]{1,0:T(8,128)(2,1)S(1)}, bf16[144,512]{1,0:T(8,128)(2,1)S(1)}) custom-call(s32[1]{0:T(128)} %bitcast.part_ref.column_ref, bf16[512,512]{1,0:T(8,128)(2,1)} %latent_ref.1, bf16[64,512]{1,0:T(8,128)(2,1)} %rope_ref.1), custom_call_target="tpu_custom_call" | custom-call | bytes 600000 | tf_op jit(solution)/shard_map/pack_part/pallas_call | solution.py:73
  1.1 3.5 %collective-permute-start.2 = (bf16[144,512]{1,0:T(8,128)(2,1)S(1)}, bf16[144,512]{1,0:T(8,128)(2,1)S(1)}, u32[]{:S(2)}, u32[]{:S(2)}) collective-permute-start(bf16[144,512]{1,0:T(8,128)(2,1)S(1)} %get-tuple-element.24), channel_id=1, source_target_pairs={{0,4},{4,8},{8,12},{1,5},{5,9},{9,13},{2,6},{6,10},{10,14},{3,7},{... | collective-permute-start | bytes 442376 | tf_op jit(solution)/shard_map/ppermute | solution.py:31
  4.6 3.5 %collective-permute-start.6 = (bf16[144,512]{1,0:T(8,128)(2,1)S(1)}, bf16[144,512]{1,0:T(8,128)(2,1)S(1)}, u32[]{:S(2)}, u32[]{:S(2)}) collective-permute-start(bf16[144,512]{1,0:T(8,128)(2,1)S(1)} %get-tuple-element.25), channel_id=1, source_target_pairs={{0,4},{4,8},{8,12},{1,5},{5,9},{9,13},{2,6},{6,10},{10,14},{3,7},{... | collective-permute-start | bytes 442376 | tf_op jit(solution)/shard_map/ppermute | solution.py:31
  8.1 1.2 %collective-permute-done.2.refs_0_ = bf16[144,512]{1,0:T(8,128)(2,1)S(1)} collective-permute-done((bf16[144,512]{1,0:T(8,128)(2,1)S(1)}, bf16[144,512]{1,0:T(8,128)(2,1)S(1)}, u32[]{:S(2)}, u32[]{:S(2)}) %collective-permute-start.2) | collective-permute-done | bytes 147488 | tf_op jit(solution)/shard_map/ppermute | solution.py:31
  9.3 0.0 collective-permute-start.16
  9.3 3.2 %collective-permute-done.6.refs_2_ = bf16[144,512]{1,0:T(8,128)(2,1)S(1)} collective-permute-done((bf16[144,512]{1,0:T(8,128)(2,1)S(1)}, bf16[144,512]{1,0:T(8,128)(2,1)S(1)}, u32[]{:S(2)}, u32[]{:S(2)}) %collective-permute-start.6) | collective-permute-done | bytes 147488 | tf_op jit(solution)/shard_map/ppermute | solution.py:31
  12.5 0.0 collective-permute-start.17
  12.5 3.5 %collective-permute-start.3 = (bf16[144,512]{1,0:T(8,128)(2,1)S(1)}, bf16[144,512]{1,0:T(8,128)(2,1)S(1)}, u32[]{:S(2)}, u32[]{:S(2)}) collective-permute-start(bf16[144,512]{1,0:T(8,128)(2,1)S(1)} %collective-permute-done.2.refs_0_), channel_id=1, source_target_pairs={{4,8},{8,12},{5,9},{9,13},{6,10},{10,14},{7,11},{11,15},{20,24},{2... | collective-permute-start | bytes 442376 | tf_op jit(solution)/shard_map/ppermute | solution.py:31
  16.0 0.3 collective-permute-start.1
  16.3 1.2 %collective-permute-done.1.refs_1_ = bf16[64,512]{1,0:T(8,128)(2,1)S(1)} collective-permute-done((bf16[64,512]{1,0:T(8,128)(2,1)}, bf16[64,512]{1,0:T(8,128)(2,1)S(1)}, u32[]{:S(2)}, u32[]{:S(2)}) %collective-permute-start.1) | collective-permute-done | bytes 65568 | tf_op jit(solution)/shard_map/ppermute | solution.py:36
  17.5 3.4 %collective-permute-start.7 = (bf16[144,512]{1,0:T(8,128)(2,1)S(1)}, bf16[144,512]{1,0:T(8,128)(2,1)S(1)}, u32[]{:S(2)}, u32[]{:S(2)}) collective-permute-start(bf16[144,512]{1,0:T(8,128)(2,1)S(1)} %collective-permute-done.6.refs_2_), channel_id=1, source_target_pairs={{4,8},{8,12},{5,9},{9,13},{6,10},{10,14},{7,11},{11,15},{20,24},{2... | collective-permute-start | bytes 442376 | tf_op jit(solution)/shard_map/ppermute | solution.py:31
  21.0 0.0 collective-permute-done.16.refs_1_
  21.0 1.6 %collective-permute-start.10 = (bf16[144,512]{1,0:T(8,128)(2,1)S(1)}, bf16[144,512]{1,0:T(8,128)(2,1)S(1)}, u32[]{:S(2)}, u32[]{:S(2)}) collective-permute-start(bf16[144,512]{1,0:T(8,128)(2,1)S(1)} %collective-permute-done.2.refs_0_), channel_id=1, source_target_pairs={{0,2},{2,0},{1,3},{3,1},{4,6},{6,4},{5,7},{7,5},{8,10},{10,8},{9,1... | collective-permute-start | bytes 442376 | tf_op jit(solution)/shard_map/ppermute | solution.py:36
  22.5 0.5 collective-permute-start.12
  23.1 0.0 collective-permute-done.3.refs_4_
  23.1 0.0 collective-permute-start.14
  23.1 1.1 %reshape.7.qrope_ref = bf16[1024,64]{1,0:T(8,128)(2,1)S(1)} reshape(bf16[128,512]{1,0:T(8,128)(2,1)} %param.7) | data formatting | bytes 262144 | tf_op jit(solution)/shard_map/reshape | solution.py:307
  24.2 0.3 collective-permute-done.7.refs_6_
  24.4 1.5 %collective-permute-start.4 = (bf16[144,512]{1,0:T(8,128)(2,1)S(1)}, bf16[144,512]{1,0:T(8,128)(2,1)S(1)}, u32[]{:S(2)}, u32[]{:S(2)}) collective-permute-start(bf16[144,512]{1,0:T(8,128)(2,1)S(1)} %collective-permute-done.3.refs_4_), channel_id=1, source_target_pairs={{0,2},{2,0},{1,3},{3,1},{4,6},{6,4},{5,7},{7,5},{8,10},{10,8},{9,1... | collective-permute-start | bytes 442376 | tf_op jit(solution)/shard_map/ppermute | solution.py:36
  25.9 1.8 %collective-permute-done.10.refs_0_ = bf16[144,512]{1,0:T(8,128)(2,1)S(1)} collective-permute-done((bf16[144,512]{1,0:T(8,128)(2,1)S(1)}, bf16[144,512]{1,0:T(8,128)(2,1)S(1)}, u32[]{:S(2)}, u32[]{:S(2)}) %collective-permute-start.10) | collective-permute-done | bytes 147488 | tf_op jit(solution)/shard_map/ppermute | solution.py:36
  27.7 0.0 collective-permute-start.15
  27.8 3.2 %collective-permute-done.12.refs_2_ = bf16[144,512]{1,0:T(8,128)(2,1)S(1)} collective-permute-done((bf16[144,512]{1,0:T(8,128)(2,1)S(1)}, bf16[144,512]{1,0:T(8,128)(2,1)S(1)}, u32[]{:S(2)}, u32[]{:S(2)}) %collective-permute-start.12) | collective-permute-done | bytes 147488 | tf_op jit(solution)/shard_map/ppermute | solution.py:36
  30.9 1.5 %collective-permute-start.8 = (bf16[144,512]{1,0:T(8,128)(2,1)S(1)}, bf16[144,512]{1,0:T(8,128)(2,1)S(1)}, u32[]{:S(2)}, u32[]{:S(2)}) collective-permute-start(bf16[144,512]{1,0:T(8,128)(2,1)S(1)} %collective-permute-done.7.refs_6_), channel_id=1, source_target_pairs={{0,2},{2,0},{1,3},{3,1},{4,6},{6,4},{5,7},{7,5},{8,10},{10,8},{9,1... | collective-permute-start | bytes 442376 | tf_op jit(solution)/shard_map/ppermute | solution.py:36
  32.4 0.0 collective-permute-done.14.refs_5_
  32.4 0.0 collective-permute-start.11
  32.4 0.0 collective-permute-done.refs_0_
  32.4 0.5 collective-permute-start.13
  32.9 5.1 %attend_own.1 = (bf16[1024,512]{1,0:T(8,128)(2,1)S(1)}, f32[1024,1]{1,0:T(8,128)S(1)}, f32[1024,1]{1,0:T(8,128)S(1)}, f32[1024,512]{1,0:T(8,128)S(1)}) custom-call(s32[1]{0:T(128)} %bitcast.1.rep_ref, bf16[1024,512]{1,0:T(8,128)(2,1)} %bitcast.6, bf16[1024,64]{1,0:T(8,128)(2,1)S(1)} %reshape.7.qrope_ref, bf16[512,512]{1,0:T(8,128)(2,1)} %latent_ref.1, ...), custom_call_target="tpu_custom_call" | custom-call | flops 2147483648 | bytes 1048576 | tf_op jit(solution)/shard_map/attend_own/pallas_call | solution.py:174
  38.1 0.0 slice-start
  38.1 2.7 %shard_map.64 = (f32[1024,1]{1,0:T(8,128)S(1)}, f32[1024,1]{1,0:T(8,128)S(1)}, f32[1024,512]{1,0:T(8,128)S(1)}) custom-call(s32[1]{0:T(128)} %bitcast.2.shard_ref, bf16[1024,512]{1,0:T(8,128)(2,1)S(1)} %get-tuple-element.23.query_ref, bf16[1024,64]{1,0:T(8,128)(2,1)S(1)} %reshape.7.qrope_ref, bf16[144,512]{1,0:T(8,128)(2,1)S(1)} %collective-permute-done.2.refs_0_, ...), custom_call_target="tpu_custom_call" | custom-call | flops 1207959552 | bytes 1048576 | tf_op jit(solution)/shard_map/pallas_call | solution.py:222
  40.8 0.1 collective-permute-start.5
  41.0 0.0 collective-permute-done.8.refs_2_
  41.0 0.4 collective-permute-start.9
  41.4 0.0 collective-permute-done.15.refs_7_
  41.4 0.0 collective-permute-done.11.refs_1_
  41.4 0.0 collective-permute-done.13.refs_3_
  41.4 0.0 slice-start.1
  41.4 0.0 copy-start
  41.4 4.4 %shard_map.65 = (f32[1024,1]{1,0:T(8,128)S(1)}, f32[1024,1]{1,0:T(8,128)S(1)}, f32[1024,512]{1,0:T(8,128)S(1)}) custom-call(s32[1]{0:T(128)} %bitcast.2.shard_ref, bf16[1024,512]{1,0:T(8,128)(2,1)S(1)} %get-tuple-element.23.query_ref, bf16[1024,64]{1,0:T(8,128)(2,1)S(1)} %reshape.7.qrope_ref, bf16[144,512]{1,0:T(8,128)(2,1)S(1)} %collective-permute-done.10.refs_0_, ...), custom_call_target="tpu_custom_call" | custom-call | flops 2415919104 | bytes 1048576 | tf_op jit(solution)/shard_map/pallas_call | solution.py:222
  45.8 0.0 collective-permute-done.9.refs_3_
  45.9 4.6 %attend_last.1 = bf16[128,3584]{1,0:T(8,128)(2,1)S(1)} custom-call(s32[1]{0:T(128)} %bitcast.part_ref.column_ref, s32[1]{0:T(128)} %bitcast.1.rep_ref, s32[1]{0:T(128)} %bitcast.2.shard_ref, bf16[1024,512]{1,0:T(8,128)(2,1)S(1)} %get-tuple-element.23.query_ref, bf16[1024,64]{1,0:T(8,128)(2,1)S(1)} %reshape.7.qrope_ref, ...), custom_call_target="tpu_custom_call" | custom-call | flops 1207959552 | bytes 1048576 | tf_op jit(solution)/shard_map/attend_last/pallas_call | solution.py:279
  50.5 0.1 collective-permute-start.18
  50.6 1.8 %collective-permute-done.18 = bf16[64,3584]{1,0:T(8,128)(2,1)S(1)} collective-permute-done((bf16[64,3584]{1,0:T(8,128)(2,1)S(1)}, bf16[64,3584]{1,0:T(8,128)(2,1)S(1)}, u32[]{:S(2)}, u32[]{:S(2)}) %collective-permute-start.18) | collective-permute-done | bytes 458784 | tf_op jit(solution)/shard_map/ppermute | solution.py:36
  52.4 0.1 add_convert_fusion.1
  52.4 0.6 collective-permute-start.19
  53.0 7.1 %collective-permute-done.19 = bf16[32,3584]{1,0:T(8,128)(2,1)S(1)} collective-permute-done((bf16[32,3584]{1,0:T(8,128)(2,1)S(1)}, bf16[32,3584]{1,0:T(8,128)(2,1)S(1)}, u32[]{:S(2)}, u32[]{:S(2)}) %collective-permute-start.19) | collective-permute-done | bytes 229408 | tf_op jit(solution)/shard_map/ppermute | solution.py:36
  60.2 0.8 %add_convert_fusion = bf16[32,3584]{1,0:T(8,128)(2,1)} fusion(bf16[32,3584]{1,0:T(8,128)(2,1)S(1)} %collective-permute-done.19, bf16[64,3584]{1,0:T(8,128)(2,1)S(1)} %collective-permute-done.18, bf16[128,3584]{1,0:T(8,128)(2,1)S(1)} %attend_last.1), kind=kLoop, calls=%fused_computation | loop fusion | flops 688128 | bytes 917504 | tf_op jit(solution)/shard_map/convert_element_type | solution.py:347
  (8 shorter events, 0.0 us)
Async XLA Ops:
  0.0 32.4 %collective-permute-start = (bf16[512,512]{1,0:T(8,128)(2,1)}, bf16[512,512]{1,0:T(8,128)(2,1)S(1)}, u32[]{:S(2)}, u32[]{:S(2)}) collective-permute-start(bf16[512,512]{1,0:T(8,128)(2,1)} %latent_ref.1), channel_id=1, source_target_pairs={{0,1},{1,0},{2,3},{3,2},{4,5},{5,4},{6,7},{7,6},{8,9},{9,8},{10,11... | collective-permute-start | bytes 1572872 | tf_op jit(solution)/shard_map/ppermute | solution.py:36
  1.1 8.2 %collective-permute-start.2 = (bf16[144,512]{1,0:T(8,128)(2,1)S(1)}, bf16[144,512]{1,0:T(8,128)(2,1)S(1)}, u32[]{:S(2)}, u32[]{:S(2)}) collective-permute-start(bf16[144,512]{1,0:T(8,128)(2,1)S(1)} %get-tuple-element.24), channel_id=1, source_target_pairs={{0,4},{4,8},{8,12},{1,5},{5,9},{9,13},{2,6},{6,10},{10,14},{3,7},{... | collective-permute-start | bytes 442376 | tf_op jit(solution)/shard_map/ppermute | solution.py:31
  4.6 7.9 %collective-permute-start.6 = (bf16[144,512]{1,0:T(8,128)(2,1)S(1)}, bf16[144,512]{1,0:T(8,128)(2,1)S(1)}, u32[]{:S(2)}, u32[]{:S(2)}) collective-permute-start(bf16[144,512]{1,0:T(8,128)(2,1)S(1)} %get-tuple-element.25), channel_id=1, source_target_pairs={{0,4},{4,8},{8,12},{1,5},{5,9},{9,13},{2,6},{6,10},{10,14},{3,7},{... | collective-permute-start | bytes 442376 | tf_op jit(solution)/shard_map/ppermute | solution.py:31
  9.3 11.7 %collective-permute-start.16 = (bf16[144,512]{1,0:T(8,128)(2,1)S(1)}, bf16[144,512]{1,0:T(8,128)(2,1)S(1)}, u32[]{:S(2)}, u32[]{:S(2)}) collective-permute-start(bf16[144,512]{1,0:T(8,128)(2,1)S(1)} %collective-permute-done.2.refs_0_), channel_id=1, source_target_pairs={{0,1},{1,0},{2,3},{3,2},{4,5},{5,4},{6,7},{7,6},{8,9},{9,8},{10,11... | collective-permute-start | bytes 442376 | tf_op jit(solution)/shard_map/ppermute | solution.py:36
  12.5 10.0 %collective-permute-start.17 = (bf16[144,512]{1,0:T(8,128)(2,1)S(1)}, bf16[144,512]{1,0:T(8,128)(2,1)S(1)}, u32[]{:S(2)}, u32[]{:S(2)}) collective-permute-start(bf16[144,512]{1,0:T(8,128)(2,1)S(1)} %collective-permute-done.6.refs_2_), channel_id=1, source_target_pairs={{0,1},{1,0},{2,3},{3,2},{4,5},{5,4},{6,7},{7,6},{8,9},{9,8},{10,11... | collective-permute-start | bytes 442376 | tf_op jit(solution)/shard_map/ppermute | solution.py:36
  12.5 10.6 %collective-permute-start.3 = (bf16[144,512]{1,0:T(8,128)(2,1)S(1)}, bf16[144,512]{1,0:T(8,128)(2,1)S(1)}, u32[]{:S(2)}, u32[]{:S(2)}) collective-permute-start(bf16[144,512]{1,0:T(8,128)(2,1)S(1)} %collective-permute-done.2.refs_0_), channel_id=1, source_target_pairs={{4,8},{8,12},{5,9},{9,13},{6,10},{10,14},{7,11},{11,15},{20,24},{2... | collective-permute-start | bytes 442376 | tf_op jit(solution)/shard_map/ppermute | solution.py:31
  16.0 1.5 %collective-permute-start.1 = (bf16[64,512]{1,0:T(8,128)(2,1)}, bf16[64,512]{1,0:T(8,128)(2,1)S(1)}, u32[]{:S(2)}, u32[]{:S(2)}) collective-permute-start(bf16[64,512]{1,0:T(8,128)(2,1)} %rope_ref.1), channel_id=1, source_target_pairs={{0,1},{1,0},{2,3},{3,2},{4,5},{5,4},{6,7},{7,6},{8,9},{9,8},{10,11... | collective-permute-start | bytes 196616 | tf_op jit(solution)/shard_map/ppermute | solution.py:36
  17.5 6.9 %collective-permute-start.7 = (bf16[144,512]{1,0:T(8,128)(2,1)S(1)}, bf16[144,512]{1,0:T(8,128)(2,1)S(1)}, u32[]{:S(2)}, u32[]{:S(2)}) collective-permute-start(bf16[144,512]{1,0:T(8,128)(2,1)S(1)} %collective-permute-done.6.refs_2_), channel_id=1, source_target_pairs={{4,8},{8,12},{5,9},{9,13},{6,10},{10,14},{7,11},{11,15},{20,24},{2... | collective-permute-start | bytes 442376 | tf_op jit(solution)/shard_map/ppermute | solution.py:31
  21.0 6.8 %collective-permute-start.10 = (bf16[144,512]{1,0:T(8,128)(2,1)S(1)}, bf16[144,512]{1,0:T(8,128)(2,1)S(1)}, u32[]{:S(2)}, u32[]{:S(2)}) collective-permute-start(bf16[144,512]{1,0:T(8,128)(2,1)S(1)} %collective-permute-done.2.refs_0_), channel_id=1, source_target_pairs={{0,2},{2,0},{1,3},{3,1},{4,6},{6,4},{5,7},{7,5},{8,10},{10,8},{9,1... | collective-permute-start | bytes 442376 | tf_op jit(solution)/shard_map/ppermute | solution.py:36
  22.5 8.4 %collective-permute-start.12 = (bf16[144,512]{1,0:T(8,128)(2,1)S(1)}, bf16[144,512]{1,0:T(8,128)(2,1)S(1)}, u32[]{:S(2)}, u32[]{:S(2)}) collective-permute-start(bf16[144,512]{1,0:T(8,128)(2,1)S(1)} %collective-permute-done.6.refs_2_), channel_id=1, source_target_pairs={{0,2},{2,0},{1,3},{3,1},{4,6},{6,4},{5,7},{7,5},{8,10},{10,8},{9,1... | collective-permute-start | bytes 442376 | tf_op jit(solution)/shard_map/ppermute | solution.py:36
  23.1 9.3 %collective-permute-start.14 = (bf16[144,512]{1,0:T(8,128)(2,1)S(1)}, bf16[144,512]{1,0:T(8,128)(2,1)S(1)}, u32[]{:S(2)}, u32[]{:S(2)}) collective-permute-start(bf16[144,512]{1,0:T(8,128)(2,1)S(1)} %collective-permute-done.3.refs_4_), channel_id=1, source_target_pairs={{0,1},{1,0},{2,3},{3,2},{4,5},{5,4},{6,7},{7,6},{8,9},{9,8},{10,11... | collective-permute-start | bytes 442376 | tf_op jit(solution)/shard_map/ppermute | solution.py:36
  24.4 16.4 %collective-permute-start.4 = (bf16[144,512]{1,0:T(8,128)(2,1)S(1)}, bf16[144,512]{1,0:T(8,128)(2,1)S(1)}, u32[]{:S(2)}, u32[]{:S(2)}) collective-permute-start(bf16[144,512]{1,0:T(8,128)(2,1)S(1)} %collective-permute-done.3.refs_4_), channel_id=1, source_target_pairs={{0,2},{2,0},{1,3},{3,1},{4,6},{6,4},{5,7},{7,5},{8,10},{10,8},{9,1... | collective-permute-start | bytes 442376 | tf_op jit(solution)/shard_map/ppermute | solution.py:36
  27.7 13.7 %collective-permute-start.15 = (bf16[144,512]{1,0:T(8,128)(2,1)S(1)}, bf16[144,512]{1,0:T(8,128)(2,1)S(1)}, u32[]{:S(2)}, u32[]{:S(2)}) collective-permute-start(bf16[144,512]{1,0:T(8,128)(2,1)S(1)} %collective-permute-done.7.refs_6_), channel_id=1, source_target_pairs={{0,1},{1,0},{2,3},{3,2},{4,5},{5,4},{6,7},{7,6},{8,9},{9,8},{10,11... | collective-permute-start | bytes 442376 | tf_op jit(solution)/shard_map/ppermute | solution.py:36
  30.9 10.1 %collective-permute-start.8 = (bf16[144,512]{1,0:T(8,128)(2,1)S(1)}, bf16[144,512]{1,0:T(8,128)(2,1)S(1)}, u32[]{:S(2)}, u32[]{:S(2)}) collective-permute-start(bf16[144,512]{1,0:T(8,128)(2,1)S(1)} %collective-permute-done.7.refs_6_), channel_id=1, source_target_pairs={{0,2},{2,0},{1,3},{3,1},{4,6},{6,4},{5,7},{7,5},{8,10},{10,8},{9,1... | collective-permute-start | bytes 442376 | tf_op jit(solution)/shard_map/ppermute | solution.py:36
  32.4 9.0 %collective-permute-start.11 = (bf16[144,512]{1,0:T(8,128)(2,1)S(1)}, bf16[144,512]{1,0:T(8,128)(2,1)S(1)}, u32[]{:S(2)}, u32[]{:S(2)}) collective-permute-start(bf16[144,512]{1,0:T(8,128)(2,1)S(1)} %collective-permute-done.10.refs_0_), channel_id=1, source_target_pairs={{0,1},{1,0},{2,3},{3,2},{4,5},{5,4},{6,7},{7,6},{8,9},{9,8},{10,11... | collective-permute-start | bytes 442376 | tf_op jit(solution)/shard_map/ppermute | solution.py:36
  32.4 9.0 %collective-permute-start.13 = (bf16[144,512]{1,0:T(8,128)(2,1)S(1)}, bf16[144,512]{1,0:T(8,128)(2,1)S(1)}, u32[]{:S(2)}, u32[]{:S(2)}) collective-permute-start(bf16[144,512]{1,0:T(8,128)(2,1)S(1)} %collective-permute-done.12.refs_2_), channel_id=1, source_target_pairs={{0,1},{1,0},{2,3},{3,2},{4,5},{5,4},{6,7},{7,6},{8,9},{9,8},{10,11... | collective-permute-start | bytes 442376 | tf_op jit(solution)/shard_map/ppermute | solution.py:36
  38.1 7.8 %slice-start = ((s8[7340032]{0:T(1024)(128)(4,1)}), s8[4194304]{0:T(1024)(128)(4,1)S(1)}, s32[]{:S(2)}) async-start(s8[7340032]{0:T(1024)(128)(4,1)} %bitcast.4), calls=%async_computation | async-start | bytes 8388608
  40.8 5.0 %collective-permute-start.5 = (bf16[144,512]{1,0:T(8,128)(2,1)S(1)}, bf16[144,512]{1,0:T(8,128)(2,1)S(1)}, u32[]{:S(2)}, u32[]{:S(2)}) collective-permute-start(bf16[144,512]{1,0:T(8,128)(2,1)S(1)} %collective-permute-done.4.refs_0_), channel_id=1, source_target_pairs={{0,1},{1,0},{2,3},{3,2},{4,5},{5,4},{6,7},{7,6},{8,9},{9,8},{10,11... | collective-permute-start | bytes 442376 | tf_op jit(solution)/shard_map/ppermute | solution.py:36
  41.0 4.9 %collective-permute-start.9 = (bf16[144,512]{1,0:T(8,128)(2,1)S(1)}, bf16[144,512]{1,0:T(8,128)(2,1)S(1)}, u32[]{:S(2)}, u32[]{:S(2)}) collective-permute-start(bf16[144,512]{1,0:T(8,128)(2,1)S(1)} %collective-permute-done.8.refs_2_), channel_id=1, source_target_pairs={{0,1},{1,0},{2,3},{3,2},{4,5},{5,4},{6,7},{7,6},{8,9},{9,8},{10,11... | collective-permute-start | bytes 442376 | tf_op jit(solution)/shard_map/ppermute | solution.py:36
  41.4 4.4 %slice-start.1 = ((s8[7340032]{0:T(1024)(128)(4,1)}), s8[3145728]{0:T(1024)(128)(4,1)S(1)}, s32[]{:S(2)}) async-start(s8[7340032]{0:T(1024)(128)(4,1)} %bitcast.4), calls=%async_computation.1 | async-start | bytes 6291456
  41.4 4.4 %copy-start = (bf16[8,512,128]{2,1,0:T(8,128)(2,1)S(1)}, bf16[8,512,128]{2,1,0:T(8,128)(2,1)}, u32[]{:S(2)}) copy-start(bf16[8,512,128]{2,1,0:T(8,128)(2,1)} %refs_7_.1) | copy-start | bytes 3145732
  50.5 1.9 %collective-permute-start.18 = (bf16[64,3584]{1,0:T(8,128)(2,1)S(1)}, bf16[64,3584]{1,0:T(8,128)(2,1)S(1)}, u32[]{:S(2)}, u32[]{:S(2)}) collective-permute-start(bf16[64,3584]{1,0:T(8,128)(2,1)S(1)} %slice.24), channel_id=1, source_target_pairs={{0,1},{1,0},{2,3},{3,2},{4,5},{5,4},{6,7},{7,6},{8,9},{9,8},{10,11... | collective-permute-start | bytes 1376264 | tf_op jit(solution)/shard_map/ppermute | solution.py:36
  52.4 7.7 %collective-permute-start.19 = (bf16[32,3584]{1,0:T(8,128)(2,1)S(1)}, bf16[32,3584]{1,0:T(8,128)(2,1)S(1)}, u32[]{:S(2)}, u32[]{:S(2)}) collective-permute-start(bf16[32,3584]{1,0:T(8,128)(2,1)S(1)} %add_convert_fusion.1), channel_id=1, source_target_pairs={{0,2},{2,0},{1,3},{3,1},{4,6},{6,4},{5,7},{7,5},{8,10},{10,8},{9,1... | collective-permute-start | bytes 688136 | tf_op jit(solution)/shard_map/ppermute | solution.py:36
